TPU v7x, 32 devices: a whole 2x2x4 slice. The times are simulated.
32 devices in a mesh: heads: 8 (over y, x, core), batch: 4 (over z).
Axes of the slice: x: 2, y: 2, z: 4, core: 2. Of those that a mesh axis runs over, the one named last changes fastest.
Arguments:
- tokens: bfloat16 [2, 4, 1024, 2048], P(None, 'batch', 'heads'), may hold values from -6 to 6
- cotangent: bfloat16 [2, 4, 1024, 2048], P(None, 'batch', 'heads'), may hold values from -6 to 6
- doc_lengths: int32 [2, 4, 4], P(None, 'batch'), may hold values from 1 to 768, 1024 in all within a row
- pad_mask: int32 [2, 4, 1024], P(None, 'batch'), may hold values 0 or 1
- w_query: bfloat16 [2048, 1024], P(None, 'heads'), may hold values from -0.1875 to 0.1875
- w_key: bfloat16 [2048, 1024], P(None, 'heads'), may hold values from -0.1875 to 0.1875
- w_value: bfloat16 [2048, 1024], P(None, 'heads'), may hold values from -0.125 to 0.125
- w_out: bfloat16 [1024, 2048], P('heads'), may hold values from -0.75 to 0.75
- w_gate: bfloat16 [2048, 8192], P(None, 'heads'), may hold values from -0.125 to 0.125
- w_up: bfloat16 [2048, 8192], P(None, 'heads'), may hold values from -0.125 to 0.125
- w_down: bfloat16 [8192, 2048], P('heads'), may hold values from -0.0625 to 0.0625
- norm_attn: float32 [2048], replicated, may hold values from 0.1 to 1.9
- norm_mlp: float32 [2048], replicated, may hold values from 0.1 to 1.9
- mix_gate: float32 [8], P('heads'), may hold values from -2 to 2
Outputs:
- layer_out: bfloat16 [2, 4, 1024, 2048], P(None, 'batch', 'heads')
- grad_tokens: float32 [2, 4, 1024, 2048], P(None, 'batch', 'heads')
- grad_w_query: float32 [2048, 1024], P(None, 'heads')
- grad_w_key: float32 [2048, 1024], P(None, 'heads')
- grad_w_value: float32 [2048, 1024], P(None, 'heads')
- grad_w_out: float32 [1024, 2048], P('heads')
- grad_w_gate: float32 [2048, 8192], P(None, 'heads')
- grad_w_up: float32 [2048, 8192], P(None, 'heads')
- grad_w_down: float32 [8192, 2048], P('heads')
- grad_norm_attn: float32 [2048], replicated
- grad_norm_mlp: float32 [2048], replicated
- grad_mix_gate: float32 [8], P('heads')
Inputs may be any that keep to these rules, and one draw needn't show every extreme that they name: `doc_lengths`: the 4 lengths of a sequence sum to 1024; the longest is 768.
All inputs are finite; a program needn't handle non-finite values. No bound on the sum of `pad_mask` on one device may be relied on, other than what follows from the above.
Results may differ from a plain program's by a relative error of at most 0.018.
Values may be sent and summed in bfloat16 or wider, within the bound.
No kernel may reach another device: no remote copies, remote signals or barrier semaphores. Data moves between devices by JAX's collectives and lax.ppermute only.
A program may use at most 256 MiB of HBM per device.

v0:
```python
import jax
import jax.numpy as jnp
from jax import lax
from jax.sharding import PartitionSpec as P

DH = 128
SEG = 512
SEGS = 2
LEN = 1024
MICRO = 2
epsilon = 1e-05
big_negative = -1e30


def dot_rows(left_mat, right_mat):
    return lax.dot_general(
        left_mat, right_mat, (((1,), (1,)), ((), ())), preferred_element_type=jnp.float32
    )


def dot_cols(left_mat, right_mat):
    return lax.dot_general(
        left_mat, right_mat, (((0,), (0,)), ((), ())), preferred_element_type=jnp.float32
    )


def batch_mm(left, right):
    return lax.dot_general(
        left, right, (((2,), (1,)), ((0,), (0,))), preferred_element_type=jnp.float32
    )


def batch_mt(left, right):
    return lax.dot_general(
        left, right, (((2,), (2,)), ((0,), (0,))), preferred_element_type=jnp.float32
    )


def batch_tm(left, right):
    return lax.dot_general(
        left, right, (((1,), (1,)), ((0,), (0,))), preferred_element_type=jnp.float32
    )


def norm_scale(row_block):
    return lax.rsqrt(jnp.mean(row_block * row_block, axis=-1, keepdims=True) + epsilon)


def norm_back(row_block, row_scale, gain_vec, upstream):
    shaped = upstream * gain_vec
    inner = jnp.mean(shaped * row_block, axis=-1, keepdims=True)
    d_rows = row_scale * shaped - row_block * row_scale * row_scale * row_scale * inner
    d_gain = jnp.sum(upstream * row_block * row_scale, axis=0)
    return (d_rows, d_gain)


def positive(values_in):
    return jnp.where(values_in > 0, values_in + 1.0, jnp.exp(values_in))


def local_mask(begin_row, positions, doc_ids, valid_keys):
    seg_pos = positions[begin_row : begin_row + SEG]
    seg_doc = doc_ids[:, begin_row : begin_row + SEG]
    seg_valid = valid_keys[:, begin_row : begin_row + SEG]
    same_doc = seg_doc[:, :, None] == seg_doc[:, None, :]
    causal = (seg_pos[None, :] <= seg_pos[:, None])[None]
    diagonal = (seg_pos[None, :] == seg_pos[:, None])[None]
    return same_doc & causal & (seg_valid[:, None, :] | diagonal)


def memory_mask(begin_row, doc_ids, valid_keys):
    seg_doc = doc_ids[:, begin_row : begin_row + SEG]
    return (seg_doc[:, :, None] == doc_ids[:, None, :begin_row]) & valid_keys[:, None, :begin_row]


def head_forward(query_all, key_all, value_all, share, positions, doc_ids, valid_keys):
    score_scale = DH ** (-0.5)
    pos_query = positive(query_all.astype(jnp.float32)).astype(jnp.bfloat16)
    pos_key = positive(key_all.astype(jnp.float32)).astype(jnp.bfloat16)
    kept = []
    dotted_parts, recalled_parts = ([], [])
    for segment in range(SEGS):
        rows = slice(segment * SEG, (segment + 1) * SEG)
        before = slice(0, segment * SEG)
        allowed = local_mask(segment * SEG, positions, doc_ids, valid_keys)
        scores = jnp.where(
            allowed, batch_mt(query_all[:, rows], key_all[:, rows]) * score_scale, big_negative
        )
        shifted = jnp.exp(scores - jnp.max(scores, axis=2, keepdims=True))
        soft_probs = shifted / jnp.sum(shifted, axis=2, keepdims=True)
        dotted_parts.append(batch_mm(soft_probs.astype(jnp.bfloat16), value_all[:, rows]))
        if segment == 0:
            recalled_parts.append(jnp.zeros((query_all.shape[0], SEG, DH), jnp.float32))
            kept.append((soft_probs,))
        else:
            mem_allowed = memory_mask(segment * SEG, doc_ids, valid_keys)
            weights = jnp.where(mem_allowed, batch_mt(pos_query[:, rows], pos_key[:, before]), 0.0)
            row_total = jnp.sum(weights, axis=2, keepdims=True)
            denominator = jnp.maximum(row_total, 1.0)
            weights_low = weights.astype(jnp.bfloat16)
            numerator = batch_mm(weights_low, value_all[:, before])
            recalled_parts.append(numerator / denominator)
            kept.append((soft_probs, mem_allowed, row_total, weights_low, numerator))
    dotted = jnp.concatenate(dotted_parts, axis=1)
    recalled = jnp.concatenate(recalled_parts, axis=1)
    mixed_head = share * recalled + (1.0 - share) * dotted
    return (mixed_head, dotted, recalled, pos_query, pos_key, kept)


def head_backward(query_all, key_all, value_all, share, d_mixed, forward_kept):
    _, dotted, recalled, pos_query, pos_key, kept = forward_kept
    score_scale = DH ** (-0.5)
    query_float = query_all.astype(jnp.float32)
    key_float = key_all.astype(jnp.float32)
    d_share = jnp.sum(d_mixed * (recalled - dotted)) * share * (1.0 - share)
    d_dotted = ((1.0 - share) * d_mixed).astype(jnp.bfloat16)
    d_recalled = share * d_mixed
    nothing = jnp.zeros((query_all.shape[0], SEG, DH), jnp.float32)
    d_query, d_key, d_value, d_posq, d_posk = [[nothing for _ in range(SEGS)] for _ in range(5)]
    for segment in range(SEGS):
        rows = slice(segment * SEG, (segment + 1) * SEG)
        before = slice(0, segment * SEG)
        soft_probs = kept[segment][0]
        d_dot_seg = d_dotted[:, rows]
        d_value[segment] += batch_tm(soft_probs.astype(jnp.bfloat16), d_dot_seg)
        d_probs = batch_mt(d_dot_seg, value_all[:, rows])
        d_scores = (
            soft_probs * (d_probs - jnp.sum(soft_probs * d_probs, axis=2, keepdims=True))
        ).astype(jnp.bfloat16)
        d_query[segment] += batch_mm(d_scores, key_all[:, rows]) * score_scale
        d_key[segment] += batch_tm(d_scores, query_all[:, rows]) * score_scale
        if segment > 0:
            _, mem_allowed, row_total, weights_low, numerator = kept[segment]
            denominator = jnp.maximum(row_total, 1.0)
            d_recall_seg = d_recalled[:, rows]
            d_numer = (d_recall_seg / denominator).astype(jnp.bfloat16)
            d_denom = jnp.where(
                row_total > 1.0,
                -jnp.sum(d_recall_seg * numerator, axis=2, keepdims=True)
                / (denominator * denominator),
                0.0,
            )
            d_weights = jnp.where(
                mem_allowed, batch_mt(d_numer, value_all[:, before]) + d_denom, 0.0
            ).astype(jnp.bfloat16)
            d_posq[segment] += batch_mm(d_weights, pos_key[:, before])
            d_posk_all = batch_tm(d_weights, pos_query[:, rows])
            d_value_all = batch_tm(weights_low, d_numer)
            for earlier in range(segment):
                part = slice(earlier * SEG, (earlier + 1) * SEG)
                d_posk[earlier] += d_posk_all[:, part]
                d_value[earlier] += d_value_all[:, part]
    d_query, d_key, d_value, d_posq, d_posk = [
        jnp.concatenate(parts, axis=1) for parts in (d_query, d_key, d_value, d_posq, d_posk)
    ]
    d_query = d_query + d_posq * jnp.where(query_float > 0, 1.0, jnp.exp(query_float))
    d_key = d_key + d_posk * jnp.where(key_float > 0, 1.0, jnp.exp(key_float))
    return (
        d_query.astype(jnp.bfloat16),
        d_key.astype(jnp.bfloat16),
        d_value.astype(jnp.bfloat16),
        d_share,
    )


class Chain:

    def __init__(self, axis, size, depth):
        self.axis, self.size, self.depth = (axis, size, depth)
        self.place = lax.axis_index(axis)
        half = size // 2
        self.stages = [("in", [(s - 1, s), (size - s, size - 1 - s)]) for s in range(1, half)]
        self.stages.append(("in", [(half - 1, half), (half, half - 1)]))
        self.stages += [
            ("out", [(s, s - 1), (size - 1 - s, size - s)]) for s in range(half - 1, 0, -1)
        ]
        self.entered = []
        self.last = [None] * len(self.stages)

    def add(self, array):
        if self.size == 1:
            return array
        if self.size % 2:
            return lax.psum(array, self.axis)
        if len(self.entered) >= self.depth:
            array, _ = lax.optimization_barrier((array, self.entered[-self.depth]))
        for number, (kind, pairs) in enumerate(self.stages):
            arrived = lax.ppermute(array, self.axis, pairs)
            if self.last[number] is not None:
                array, arrived, _ = lax.optimization_barrier((array, arrived, self.last[number]))
            if kind == "in":
                array = array + arrived
            else:
                receives = jnp.zeros((), jnp.bool_)
                for _, target in pairs:
                    receives = receives | (self.place == target)
                array = jnp.where(receives, arrived, array)
            self.last[number] = array
            if number == 0:
                self.entered.append(array)
        return array


def per_device(
    tokens,
    cotangent,
    doc_lengths,
    pad_mask,
    w_query,
    w_key,
    w_value,
    w_out,
    w_gate,
    w_up,
    w_down,
    norm_attn,
    norm_mlp,
    mix_gate,
    *,
    n_heads,
    n_batch
):
    width = tokens.shape[-1]
    rows = tokens.shape[2]
    own_rows = MICRO * rows
    all_rows = n_heads * own_rows
    hidden_cols = w_gate.shape[1]
    here = lax.axis_index("heads")
    low = jnp.bfloat16

    def by_sequence(array):
        cols = array.shape[-1]
        return (
            array.reshape(n_heads, MICRO, rows, cols)
            .transpose(1, 0, 2, 3)
            .reshape(MICRO, LEN, cols)
        )

    def by_device(array):
        cols = array.shape[-1]
        return (
            array.reshape(MICRO, n_heads, rows, cols).transpose(1, 0, 2, 3).reshape(all_rows, cols)
        )

    def gather(array):
        return lax.all_gather(array, "heads", axis=0, tiled=True)

    def scatter(array):
        return lax.psum_scatter(array, "heads", scatter_dimension=0, tiled=True)

    def own(array):
        return lax.dynamic_slice_in_dim(array, here * own_rows, own_rows, 0)

    w_qkv = jnp.concatenate([w_query, w_key, w_value], axis=1)
    w_gate_up = jnp.concatenate([w_gate, w_up], axis=1)
    share = jax.nn.sigmoid(mix_gate)[0]
    positions = jnp.arange(LEN, dtype=jnp.int32)
    doc_ends = jnp.cumsum(doc_lengths[:, 0], axis=1)
    doc_ids = jnp.sum((positions[None, :, None] >= doc_ends[:, None, :]).astype(jnp.int32), axis=2)
    valid_keys = pad_mask[:, 0] == 1
    tok_own = tokens.reshape(own_rows, width)
    cot_own = cotangent.reshape(own_rows, width)
    tok_all = gather(tok_own)
    w_out_all = gather(w_out)
    x_all = tok_all.astype(jnp.float32)
    h1_all = (x_all * norm_scale(x_all) * norm_attn).astype(low)
    qkv = jnp.dot(h1_all, w_qkv, preferred_element_type=jnp.float32).astype(low)
    query, key, value = [by_sequence(qkv[:, i * DH : (i + 1) * DH]) for i in range(3)]
    head_kept = head_forward(query, key, value, share, positions, doc_ids, valid_keys)
    mixed = by_device(head_kept[0].astype(low))
    mixed_all = lax.all_gather(mixed, "heads", axis=1, tiled=True)
    cot_all = gather(cot_own)
    y1_all = x_all + jnp.dot(mixed_all, w_out_all, preferred_element_type=jnp.float32)
    h2_all = (y1_all * norm_scale(y1_all) * norm_mlp).astype(low)
    x_own = tok_own.astype(jnp.float32)
    y1_own = own(y1_all)
    gate_up = jnp.dot(h2_all, w_gate_up, preferred_element_type=jnp.float32)
    gate_pre = gate_up[:, :hidden_cols]
    up_pre = gate_up[:, hidden_cols:]
    sig_gate = jax.nn.sigmoid(gate_pre)
    hidden = (gate_pre * sig_gate * up_pre).astype(low)
    d_hidden = dot_rows(cot_all, w_down)
    d_up = d_hidden * gate_pre * sig_gate
    d_gate = d_hidden * up_pre * sig_gate * (1.0 + gate_pre * (1.0 - sig_gate))
    d_gate_up = jnp.concatenate([d_gate, d_up], axis=1).astype(low)
    chain = Chain("batch", n_batch, 3)
    d_h2 = scatter(dot_rows(d_gate_up, w_gate_up).astype(low)).astype(jnp.float32)
    down_parts, gate_up_parts = ([], [])
    step = hidden_cols // 4
    for begin in range(0, hidden_cols, step):
        down_parts.append(chain.add(dot_cols(hidden[:, begin : begin + step], cot_all).astype(low)))
    step = width // 8
    for begin in range(0, width, step):
        gate_up_parts.append(
            chain.add(dot_cols(h2_all[:, begin : begin + step], d_gate_up).astype(low))
        )
    mlp_own = scatter(jnp.dot(hidden, w_down, preferred_element_type=jnp.float32).astype(low))
    layer_out = (y1_own + mlp_own.astype(jnp.float32)).astype(low)
    scale_mlp = norm_scale(y1_own)
    d_y1, gain_mlp_part = norm_back(y1_own, scale_mlp, norm_mlp, d_h2)
    d_y1 = d_y1 + cot_own.astype(jnp.float32)
    d_attn = d_y1.astype(low)
    d_mixed_own = dot_rows(d_attn, w_out_all).astype(low)
    d_mixed = lax.all_to_all(d_mixed_own, "heads", split_axis=1, concat_axis=0, tiled=True)
    grad_out = scatter(dot_cols(own(mixed_all), d_attn).astype(low))
    d_query, d_key, d_value, d_share = head_backward(
        query, key, value, share, by_sequence(d_mixed).astype(jnp.float32), head_kept
    )
    d_qkv = jnp.concatenate([by_device(d_query), by_device(d_key), by_device(d_value)], axis=1)
    d_h1 = scatter(dot_rows(d_qkv, w_qkv).astype(low)).astype(jnp.float32)
    grad_out = chain.add(grad_out)
    grad_qkv = chain.add(dot_cols(h1_all, d_qkv).astype(low))
    d_x, gain_attn_part = norm_back(x_own, norm_scale(x_own), norm_attn, d_h1)
    grad_tokens = (d_x + d_y1).reshape(tokens.shape)
    slots = jnp.where(jnp.arange(n_heads) == here, d_share, 0.0)
    sums = lax.psum(jnp.concatenate([gain_attn_part, gain_mlp_part, slots]), ("heads", "batch"))
    grad_mix = lax.dynamic_slice_in_dim(sums, 2 * width + here, 1, 0)
    wide = jnp.float32
    grad_qkv = grad_qkv.astype(wide)
    grad_gate_up = jnp.concatenate([p.astype(wide) for p in gate_up_parts], axis=0)
    grad_down = jnp.concatenate([p.astype(wide) for p in down_parts], axis=0)
    return (
        layer_out.reshape(tokens.shape),
        grad_tokens,
        grad_qkv[:, :DH],
        grad_qkv[:, DH : 2 * DH],
        grad_qkv[:, 2 * DH :],
        grad_out.astype(wide),
        grad_gate_up[:, :hidden_cols],
        grad_gate_up[:, hidden_cols:],
        grad_down,
        sums[:width],
        sums[width : 2 * width],
        grad_mix,
    )


def solution(mesh):
    in_specs = (
        P(None, "batch", "heads", None),
        P(None, "batch", "heads", None),
        P(None, "batch", None),
        P(None, "batch", None),
        P(None, "heads"),
        P(None, "heads"),
        P(None, "heads"),
        P("heads", None),
        P(None, "heads"),
        P(None, "heads"),
        P("heads", None),
        P(),
        P(),
        P("heads"),
    )
    out_specs = (
        P(None, "batch", "heads", None),
        P(None, "batch", "heads", None),
        P(None, "heads"),
        P(None, "heads"),
        P(None, "heads"),
        P("heads", None),
        P(None, "heads"),
        P(None, "heads"),
        P("heads", None),
        P(),
        P(),
        P("heads"),
    )

    def program(*arrays):
        return per_device(*arrays, n_heads=mesh.shape["heads"], n_batch=mesh.shape["batch"])

    return jax.shard_map(
        program, mesh=mesh, in_specs=in_specs, out_specs=out_specs, check_vma=False
    )
```

profile of v0, /device:TPU:0, one launch (start us, length us, event | category | flops | bytes accessed | tf_op | source)
XLA Modules:
  0.0 852.9 jit_solution(9633711189530872917)
XLA Ops:
  16.1 50.9 %all-gather.5.cloned.1.call-done = bf16[2048,2048]{1,0:T(8,128)(2,1)} async-done(((bf16[256,2048]{1,0:T(8,128)(2,1)}), bf16[2048,2048]{1,0:T(8,128)(2,1)}) %all-gather.5.cloned.1.call-update) | async-done | bytes 8388624 | tf_op jit(solution)/shard_map/all_gather | solution.py:246
  67.0 5.2 fusion.2
  72.8 4.8 convolution_convert_fusion.5
  87.3 2.9 fusion.56
  93.2 4.8 constant_dynamic-update-slice_fusion.4
  100.5 5.2 all-gather.9.cloned.1.call-done
  105.7 39.9 %all-gather.7.cloned.1.call-done = bf16[2048,1024]{1,0:T(8,128)(2,1)} async-done(((bf16[2048,128]{1,0:T(8,128)(2,1)}), bf16[2048,1024]{1,0:T(8,128)(2,1)}) %all-gather.7.cloned.1.call-update) | async-done | bytes 4194320 | tf_op jit(solution)/shard_map/all_gather | solution.py:271
  145.6 13.5 %multiply_reduce_fusion = (f32[2048]{0:T(1024)S(1)}, f32[2048,2048]{1,0:T(8,128)S(1)}) fusion(bf16[2048,1024]{1,0:T(8,128)(2,1)} %all-gather.7.cloned.1.call-done, bf16[1024,2048]{1,0:T(8,128)(2,1)} %all-gather.9.cloned.1.call-done, bf16[2048,2048]{1,0:T(8,128)(2,1)} %all-gather.5.cloned.1.call-done), kind=kOutput, calls=%fused_computation.9 | convolution fusion | flops 8606709760 | bytes 33562624 | tf_op jit(solution)/shard_map/dot_general | solution.py:273
  159.1 5.8 copy-done
  164.9 4.4 multiply_convert_fusion
  169.3 24.3 %fusion.125 = f32[2048,2048]{0,1:T(8,128)} fusion(bf16[2048,2048]{1,0:T(8,128)(2,1)} %multiply_convert_fusion, bf16[2048,2048]{1,0:T(8,128)(2,1)} %constant_dynamic-update-slice_fusion.3), kind=kOutput, calls=%fused_computation.223 | convolution fusion | flops 17179869184 | bytes 33554432 | tf_op jit(solution)/shard_map/dot_general | solution.py:277
  193.7 8.1 all-gather.11.cloned.1.call-done
  201.8 22.8 %multiply_convert_fusion.2 = (bf16[2048,1024]{0,1:T(8,128)(2,1)S(1)}, bf16[2048,1024]{0,1:T(8,128)(2,1)}, bf16[2048,1024]{0,1:T(8,128)(2,1)}) fusion(f32[2048,2048]{0,1:T(8,128)} %fusion.125, bf16[2048,2048]{1,0:T(8,128)(2,1)} %all-gather.11.cloned.1.call-done, bf16[1024,2048]{1,0:T(8,128)(2,1)} %param.24), kind=kOutput, calls=%fused_computation.12 | convolution fusion | flops 8623489024 | bytes 41943040 | tf_op jit(solution)/shard_map/dot_general | solution.py:16
  226.6 22.9 %convolution_convert_fusion.1 = bf16[2048,2048]{1,0:T(8,128)(2,1)} fusion(bf16[2048,2048]{1,0:T(8,128)(2,1)} %constant_dynamic-update-slice_fusion.3, bf16[2048,1024]{0,1:T(8,128)(2,1)} %get-tuple-element.249, bf16[2048,1024]{0,1:T(8,128)(2,1)S(1)} %get-tuple-element.248), kind=kOutput, calls=%fused_computation.16 | convolution fusion | flops 17200840704 | bytes 25165824 | tf_op jit(solution)/shard_map/dot_general | solution.py:16
  249.6 14.5 %convolution_convert_fusion.2 = bf16[2048,2048]{1,0:T(8,128)(2,1)} fusion(bf16[2048,1024]{0,1:T(8,128)(2,1)} %get-tuple-element.252, bf16[1024,2048]{1,0:T(8,128)(2,1)} %param.24), kind=kOutput, calls=%fused_computation.17 | convolution fusion | flops 8594128896 | bytes 16777216 | tf_op jit(solution)/shard_map/dot_general | solution.py:297
  266.3 6.2 convolution_convert_fusion.13
  272.6 3.9 collective-permute-start.1
  276.5 6.4 convolution_convert_fusion.14
  285.5 3.4 convolution_convert_fusion.15
  288.9 3.4 convolution_convert_fusion.9
  292.4 5.7 convolution_convert_fusion.10
  298.1 7.1 convolution_convert_fusion.16
  305.2 4.9 convolution_convert_fusion.11
  310.1 7.2 convolution_convert_fusion.7
  321.4 4.5 convolution_convert_fusion.12
  331.0 3.4 collective-permute-start.3
  336.7 3.1 fusion.16
  339.8 56.7 %reduce-scatter.5.cloned.1.call-done = bf16[256,2048]{1,0:T(8,128)(2,1)} async-done(((bf16[2048,2048]{1,0:T(8,128)(2,1)}), bf16[256,2048]{1,0:T(8,128)(2,1)}) %reduce-scatter.5.cloned.1.call-update) | async-done | bytes 1048592 | tf_op jit(solution)/shard_map/reduce_scatter | solution.py:249
  396.6 4.6 fusion.13
  403.4 4.2 all-to-all-start
  407.6 7.1 convolution_convert_fusion.8
  414.7 3.0 add.211
  419.3 6.1 collective-permute-start.7
  429.6 2.9 add.224
  437.4 2.9 add.213
  440.3 4.3 convolution_convert_fusion.3
  460.1 6.8 convolution_convert_fusion
  468.1 6.6 convolution_convert_fusion.17
  481.1 11.4 %collective-permute-start.6 = (bf16[256,2048]{1,0:T(8,128)(2,1)S(1)}, bf16[256,2048]{1,0:T(8,128)(2,1)S(1)}, u32[]{:S(2)}, u32[]{:S(2)}) collective-permute-start(bf16[256,2048]{1,0:T(8,128)(2,1)S(1)} %copy-done.22), channel_id=1, source_target_pairs={{0,1},{3,2},{4,5},{7,6},{8,9},{11,10},{12,13},{15,14},{16,17},{19,... | collective-permute-start | bytes 3145736 | tf_op jit(solution)/shard_map/ppermute | solution.py:188
  493.8 5.0 convolution_convert_fusion.6
  498.8 3.8 collective-permute-start.10
  507.4 8.6 %collective-permute-done.6 = bf16[256,2048]{1,0:T(8,128)(2,1)S(1)} collective-permute-done((bf16[256,2048]{1,0:T(8,128)(2,1)S(1)}, bf16[256,2048]{1,0:T(8,128)(2,1)S(1)}, u32[]{:S(2)}, u32[]{:S(2)}) %collective-permute-start.6) | collective-permute-done | bytes 1048608 | tf_op jit(solution)/shard_map/ppermute | solution.py:188
  519.4 19.1 %collective-permute-done.5 = bf16[256,2048]{1,0:T(8,128)(2,1)S(1)} collective-permute-done((bf16[256,2048]{1,0:T(8,128)(2,1)S(1)}, bf16[256,2048]{1,0:T(8,128)(2,1)S(1)}, u32[]{:S(2)}, u32[]{:S(2)}) %collective-permute-start.5) | collective-permute-done | bytes 1048608 | tf_op jit(solution)/shard_map/ppermute | solution.py:188
  540.9 18.1 %collective-permute-done.10 = bf16[256,2048]{1,0:T(8,128)(2,1)S(1)} collective-permute-done((bf16[256,2048]{1,0:T(8,128)(2,1)S(1)}, bf16[256,2048]{1,0:T(8,128)(2,1)S(1)}, u32[]{:S(2)}, u32[]{:S(2)}) %collective-permute-start.10) | collective-permute-done | bytes 1048608 | tf_op jit(solution)/shard_map/ppermute | solution.py:188
  561.0 8.7 %collective-permute-done.37 = bf16[256,2048]{1,0:T(8,128)(2,1)S(1)} collective-permute-done((bf16[256,2048]{1,0:T(8,128)(2,1)S(1)}, bf16[256,2048]{1,0:T(8,128)(2,1)S(1)}, u32[]{:S(2)}, u32[]{:S(2)}) %collective-permute-start.37) | collective-permute-done | bytes 1048608 | tf_op jit(solution)/shard_map/ppermute | solution.py:188
  571.2 19.0 %collective-permute-done.36 = bf16[256,2048]{1,0:T(8,128)(2,1)S(1)} collective-permute-done((bf16[256,2048]{1,0:T(8,128)(2,1)S(1)}, bf16[256,2048]{1,0:T(8,128)(2,1)S(1)}, u32[]{:S(2)}, u32[]{:S(2)}) %collective-permute-start.36) | collective-permute-done | bytes 1048608 | tf_op jit(solution)/shard_map/ppermute | solution.py:188
  600.2 14.9 %collective-permute-done.8 = bf16[256,2048]{1,0:T(8,128)(2,1)S(1)} collective-permute-done((bf16[256,2048]{1,0:T(8,128)(2,1)S(1)}, bf16[256,2048]{1,0:T(8,128)(2,1)S(1)}, u32[]{:S(2)}, u32[]{:S(2)}) %collective-permute-start.8) | collective-permute-done | bytes 1048608 | tf_op jit(solution)/shard_map/ppermute | solution.py:188
  616.3 18.6 %collective-permute-done.13 = bf16[256,2048]{1,0:T(8,128)(2,1)S(1)} collective-permute-done((bf16[256,2048]{1,0:T(8,128)(2,1)S(1)}, bf16[256,2048]{1,0:T(8,128)(2,1)S(1)}, u32[]{:S(2)}, u32[]{:S(2)}) %collective-permute-start.13) | collective-permute-done | bytes 1048608 | tf_op jit(solution)/shard_map/ppermute | solution.py:188
  636.1 4.6 maximum_convert_fusion
  642.9 6.4 convolution_convert_fusion.4
  649.3 9.9 %collective-permute-start.11 = (bf16[2048,384]{1,0:T(8,128)(2,1)}, bf16[2048,384]{1,0:T(8,128)(2,1)}, u32[]{:S(2)}, u32[]{:S(2)}) collective-permute-start(bf16[2048,384]{1,0:T(8,128)(2,1)} %convolution_convert_fusion.4), channel_id=1, source_target_pairs={{0,1},{3,2},{4,5},{7,6},{8,9},{11,10},{12,13},{15,14},{16,17},{19,... | collective-permute-start | bytes 4718600 | tf_op jit(solution)/shard_map/ppermute | solution.py:188
  670.1 19.9 %collective-permute-start.12 = (bf16[128,2048]{1,0:T(8,128)(2,1)}, bf16[128,2048]{1,0:T(8,128)(2,1)S(1)}, u32[]{:S(2)}, u32[]{:S(2)}) collective-permute-start(bf16[128,2048]{1,0:T(8,128)(2,1)} %reduce-scatter.11.cloned.1.call-done), channel_id=1, source_target_pairs={{0,1},{3,2},{4,5},{7,6},{8,9},{11,10},{12,13},{15,14},{16,17},{19,... | collective-permute-start | bytes 1572872 | tf_op jit(solution)/shard_map/ppermute | solution.py:188
  690.0 2.6 constant_dynamic-update-slice_fusion.8
  692.7 7.6 collective-permute-done.12
  704.5 2.6 constant_dynamic-update-slice_fusion.7
  707.2 5.6 collective-permute-done.31
  712.8 2.6 constant_dynamic-update-slice_fusion.6
  715.4 15.5 %collective-permute-done.30 = bf16[256,2048]{1,0:T(8,128)(2,1)} collective-permute-done((bf16[256,2048]{1,0:T(8,128)(2,1)}, bf16[256,2048]{1,0:T(8,128)(2,1)}, u32[]{:S(2)}, u32[]{:S(2)}) %collective-permute-start.30) | collective-permute-done | bytes 1048608 | tf_op jit(solution)/shard_map/ppermute | solution.py:188
  731.6 2.6 constant_dynamic-update-slice_fusion.5
  738.5 11.8 %fusion.109 = (f32[2048,1024]{1,0:T(8,128)}, f32[2048,1024]{1,0:T(8,128)}) fusion(bf16[2048,2048]{1,0:T(8,128)(2,1)} %constant_dynamic-update-slice_fusion.5), kind=kLoop, calls=%fused_computation.215 | loop fusion | bytes 33554432 | tf_op jit(solution)/shard_map/slice | solution.py:330
  751.0 16.7 %collective-permute-done.29 = bf16[128,2048]{1,0:T(8,128)(2,1)S(1)} collective-permute-done((bf16[128,2048]{1,0:T(8,128)(2,1)S(1)}, bf16[128,2048]{1,0:T(8,128)(2,1)S(1)}, u32[]{:S(2)}, u32[]{:S(2)}) %collective-permute-start.29) | collective-permute-done | bytes 524320 | tf_op jit(solution)/shard_map/ppermute | solution.py:188
  768.8 29.0 %collective-permute-done.28 = bf16[2048,384]{1,0:T(8,128)(2,1)} collective-permute-done((bf16[2048,384]{1,0:T(8,128)(2,1)}, bf16[2048,384]{1,0:T(8,128)(2,1)}, u32[]{:S(2)}, u32[]{:S(2)}) %collective-permute-start.28) | collective-permute-done | bytes 1572896 | tf_op jit(solution)/shard_map/ppermute | solution.py:188
  803.1 38.3 %psum.7 = f32[4104]{0:T(1024)S(1)} all-reduce(f32[4104]{0:T(1024)S(1)} %pad_maximum_fusion.6), channel_id=1, replica_groups=mesh['heads'=8,'batch'=4] {'heads','batch'}, use_global_device_ids=true, to_apply=%region_23.24 | all-reduce | flops 4104 | bytes 32832 | tf_op jit(solution)/shard_map/psum | solution.py:316
  842.5 3.3 fusion.11
  (344 shorter events, 134.3 us)
Async XLA Ops:
  7.2 59.8 %all-gather.5.cloned.1.call-start = ((), (), s32[]{:S(2)}) async-start(), calls=%async_computation.5 | async-start | bytes 9437184 | tf_op jit(solution)/shard_map/all_gather | solution.py:246
  7.9 97.7 %all-gather.9.cloned.1.call-start = ((), (), s32[]{:S(2)}) async-start(), calls=%async_computation.7 | async-start | bytes 4718592 | tf_op jit(solution)/shard_map/all_gather | solution.py:246
  8.7 136.9 %all-gather.7.cloned.1.call-start = ((), (), s32[]{:S(2)}) async-start(), calls=%async_computation.6 | async-start | bytes 4718592 | tf_op jit(solution)/shard_map/all_gather | solution.py:271
  10.8 71.9 %copy-start.56 = (s32[2,512]{1,0:T(2,128)}, s32[2,512]{1,0:T(2,128)S(1)}, u32[]{:S(2)}) copy-start(s32[2,512]{1,0:T(2,128)S(1)} %get-tuple-element.266) | copy-start | bytes 12292
  10.8 74.2 %copy-start.54 = (s32[2,512]{1,0:T(2,128)}, s32[2,512]{1,0:T(2,128)S(1)}, u32[]{:S(2)}) copy-start(s32[2,512]{1,0:T(2,128)S(1)} %get-tuple-element.265) | copy-start | bytes 12292
  13.5 69.2 %copy-start.58 = (pred[2,512]{1,0:T(4,128)(4,1)}, pred[2,512]{1,0:T(4,128)(4,1)S(1)}, u32[]{:S(2)}) copy-start(pred[2,512]{1,0:T(4,128)(4,1)S(1)} %get-tuple-element.268) | copy-start | bytes 3076
  14.7 57.6 %copy-start.37 = (bf16[2048,384]{1,0:T(8,128)(2,1)}, bf16[2048,384]{1,0:T(8,128)(2,1)S(1)}, u32[]{:S(2)}) copy-start(bf16[2048,384]{1,0:T(8,128)(2,1)S(1)} %constant_dynamic-update-slice_fusion) | copy-start | bytes 4718596
  16.1 56.1 %copy-start.41 = (f32[2048]{0:T(1024)S(1)}, f32[2048]{0:T(1024)}, u32[]{:S(2)}) copy-start(f32[2048]{0:T(1024)} %param.25) | copy-start | bytes 24580
  92.6 109.2 %all-gather.11.cloned.1.call-start = ((), (), s32[]{:S(2)}) async-start(), calls=%async_computation.9 | async-start | bytes 9437184 | tf_op jit(solution)/shard_map/all_gather | solution.py:246
  93.2 243.6 %reduce-scatter.7.cloned.1.call-start = ((), (), s32[]{:S(2)}) async-start(), calls=%async_computation.10 | async-start | bytes 9437184 | tf_op jit(solution)/shard_map/reduce_scatter | solution.py:249
  100.5 64.4 %copy-start.39 = (f32[2048]{0:T(1024)S(1)}, f32[2048]{0:T(1024)}, u32[]{:S(2)}) copy-start(f32[2048]{0:T(1024)} %param.26) | copy-start | bytes 24580
  249.5 147.0 %reduce-scatter.5.cloned.1.call-start = ((), (), s32[]{:S(2)}) async-start(), calls=%async_computation.8 | async-start | bytes 9437184 | tf_op jit(solution)/shard_map/reduce_scatter | solution.py:249
  266.3 19.2 %slice-start.2 = ((s8[8388608]{0:T(1024)(128)(4,1)}), s8[4194304]{0:T(1024)(128)(4,1)S(1)}, s32[]{:S(2)}) async-start(s8[8388608]{0:T(1024)(128)(4,1)} %bitcast.109), calls=%async_computation.15 | async-start | bytes 8388608
  272.5 13.0 %slice-start.3 = ((s8[8388608]{0:T(1024)(128)(4,1)}), s8[4194304]{0:T(1024)(128)(4,1)S(1)}, s32[]{:S(2)}) async-start(s8[8388608]{0:T(1024)(128)(4,1)} %bitcast.109), calls=%async_computation.16 | async-start | bytes 8388608
  272.6 53.3 %collective-permute-start.1 = (bf16[256,2048]{1,0:T(8,128)(2,1)S(1)}, bf16[256,2048]{1,0:T(8,128)(2,1)S(1)}, u32[]{:S(2)}, u32[]{:S(2)}) collective-permute-start(bf16[256,2048]{1,0:T(8,128)(2,1)S(1)} %convolution_convert_fusion.13), channel_id=1, source_target_pairs={{0,1},{3,2},{4,5},{7,6},{8,9},{11,10},{12,13},{15,14},{16,17},{19,... | collective-permute-start | bytes 3145736 | tf_op jit(solution)/shard_map/ppermute | solution.py:188
  282.9 45.1 %collective-permute-start = (bf16[256,2048]{1,0:T(8,128)(2,1)S(1)}, bf16[256,2048]{1,0:T(8,128)(2,1)S(1)}, u32[]{:S(2)}, u32[]{:S(2)}) collective-permute-start(bf16[256,2048]{1,0:T(8,128)(2,1)S(1)} %convolution_convert_fusion.14), channel_id=1, source_target_pairs={{0,1},{3,2},{4,5},{7,6},{8,9},{11,10},{12,13},{15,14},{16,17},{19,... | collective-permute-start | bytes 3145736 | tf_op jit(solution)/shard_map/ppermute | solution.py:188
  317.2 97.5 %collective-permute-start.4 = (bf16[256,2048]{1,0:T(8,128)(2,1)}, bf16[256,2048]{1,0:T(8,128)(2,1)}, u32[]{:S(2)}, u32[]{:S(2)}) collective-permute-start(bf16[256,2048]{1,0:T(8,128)(2,1)} %convolution_convert_fusion.11), channel_id=1, source_target_pairs={{0,1},{3,2},{4,5},{7,6},{8,9},{11,10},{12,13},{15,14},{16,17},{19,... | collective-permute-start | bytes 3145736 | tf_op jit(solution)/shard_map/ppermute | solution.py:188
  326.4 93.0 %collective-permute-start.27 = (bf16[256,2048]{1,0:T(8,128)(2,1)S(1)}, bf16[256,2048]{1,0:T(8,128)(2,1)}, u32[]{:S(2)}, u32[]{:S(2)}) collective-permute-start(bf16[256,2048]{1,0:T(8,128)(2,1)S(1)} %add.209), channel_id=1, source_target_pairs={{1,2},{2,1},{5,6},{6,5},{9,10},{10,9},{13,14},{14,13},{17,18},{18,... | collective-permute-start | bytes 3145736 | tf_op jit(solution)/shard_map/ppermute | solution.py:188
  329.4 98.7 %collective-permute-start.26 = (bf16[256,2048]{1,0:T(8,128)(2,1)}, bf16[256,2048]{1,0:T(8,128)(2,1)}, u32[]{:S(2)}, u32[]{:S(2)}) collective-permute-start(bf16[256,2048]{1,0:T(8,128)(2,1)} %add.210), channel_id=1, source_target_pairs={{1,2},{2,1},{5,6},{6,5},{9,10},{10,9},{13,14},{14,13},{17,18},{18,... | collective-permute-start | bytes 3145736 | tf_op jit(solution)/shard_map/ppermute | solution.py:188
  331.0 101.5 %collective-permute-start.3 = (bf16[256,2048]{1,0:T(8,128)(2,1)}, bf16[256,2048]{1,0:T(8,128)(2,1)}, u32[]{:S(2)}, u32[]{:S(2)}) collective-permute-start(bf16[256,2048]{1,0:T(8,128)(2,1)} %convolution_convert_fusion.12), channel_id=1, source_target_pairs={{0,1},{3,2},{4,5},{7,6},{8,9},{11,10},{12,13},{15,14},{16,17},{19,... | collective-permute-start | bytes 3145736 | tf_op jit(solution)/shard_map/ppermute | solution.py:188
  334.4 101.3 %collective-permute-start.2 = (bf16[256,2048]{1,0:T(8,128)(2,1)}, bf16[256,2048]{1,0:T(8,128)(2,1)}, u32[]{:S(2)}, u32[]{:S(2)}) collective-permute-start(bf16[256,2048]{1,0:T(8,128)(2,1)} %convolution_convert_fusion.15), channel_id=1, source_target_pairs={{0,1},{3,2},{4,5},{7,6},{8,9},{11,10},{12,13},{15,14},{16,17},{19,... | collective-permute-start | bytes 3145736 | tf_op jit(solution)/shard_map/ppermute | solution.py:188
  403.4 41.4 %all-to-all-start = ((bf16[256,8,128]{2,0,1:T(8,128)(2,1)}), bf16[256,8,128]{2,0,1:T(8,128)(2,1)}, u32[]{:S(2)}, u32[]{:S(2)}) async-start(bf16[256,8,128]{2,0,1:T(8,128)(2,1)} %bitcast.119), calls=%async_computation.2 | async-start | bytes 1048576 | tf_op jit(solution)/shard_map/all_to_all | solution.py:304
  407.5 262.6 %reduce-scatter.11.cloned.1.call-start = ((), (), s32[]{:S(2)}) async-start(), calls=%async_computation.12 | async-start | bytes 4718592 | tf_op jit(solution)/shard_map/reduce_scatter | solution.py:249
  417.7 49.3 %collective-permute-start.25 = (bf16[256,2048]{1,0:T(8,128)(2,1)}, bf16[256,2048]{1,0:T(8,128)(2,1)}, u32[]{:S(2)}, u32[]{:S(2)}) collective-permute-start(bf16[256,2048]{1,0:T(8,128)(2,1)} %add.211), channel_id=1, source_target_pairs={{1,2},{2,1},{5,6},{6,5},{9,10},{10,9},{13,14},{14,13},{17,18},{18,... | collective-permute-start | bytes 3145736 | tf_op jit(solution)/shard_map/ppermute | solution.py:188
  419.3 57.5 %collective-permute-start.7 = (bf16[256,2048]{1,0:T(8,128)(2,1)}, bf16[256,2048]{1,0:T(8,128)(2,1)}, u32[]{:S(2)}, u32[]{:S(2)}) collective-permute-start(bf16[256,2048]{1,0:T(8,128)(2,1)} %convolution_convert_fusion.9), channel_id=1, source_target_pairs={{0,1},{3,2},{4,5},{7,6},{8,9},{11,10},{12,13},{15,14},{16,17},{19,... | collective-permute-start | bytes 3145736 | tf_op jit(solution)/shard_map/ppermute | solution.py:188
  428.1 52.1 %collective-permute-start.41 = (bf16[256,2048]{1,0:T(8,128)(2,1)}, bf16[256,2048]{1,0:T(8,128)(2,1)}, u32[]{:S(2)}, u32[]{:S(2)}) collective-permute-start(bf16[256,2048]{1,0:T(8,128)(2,1)} %add.223), channel_id=1, source_target_pairs={{1,0},{2,3},{5,4},{6,7},{9,8},{10,11},{13,12},{14,15},{17,16},{18,... | collective-permute-start | bytes 3145736 | tf_op jit(solution)/shard_map/ppermute | solution.py:188
  432.5 48.6 %collective-permute-start.40 = (bf16[256,2048]{1,0:T(8,128)(2,1)}, bf16[256,2048]{1,0:T(8,128)(2,1)}, u32[]{:S(2)}, u32[]{:S(2)}) collective-permute-start(bf16[256,2048]{1,0:T(8,128)(2,1)} %add.224), channel_id=1, source_target_pairs={{1,0},{2,3},{5,4},{6,7},{9,8},{10,11},{13,12},{14,15},{17,16},{18,... | collective-permute-start | bytes 3145736 | tf_op jit(solution)/shard_map/ppermute | solution.py:188
  435.7 56.8 %collective-permute-start.24 = (bf16[256,2048]{1,0:T(8,128)(2,1)S(1)}, bf16[256,2048]{1,0:T(8,128)(2,1)}, u32[]{:S(2)}, u32[]{:S(2)}) collective-permute-start(bf16[256,2048]{1,0:T(8,128)(2,1)S(1)} %add.212), channel_id=1, source_target_pairs={{1,2},{2,1},{5,6},{6,5},{9,10},{10,9},{13,14},{14,13},{17,18},{18,... | collective-permute-start | bytes 3145736 | tf_op jit(solution)/shard_map/ppermute | solution.py:188
  444.7 356.5 %reduce-scatter.9.cloned.1.call-start = ((), (), s32[]{:S(2)}) async-start(), calls=%async_computation.11 | async-start | bytes 9437184 | tf_op jit(solution)/shard_map/reduce_scatter | solution.py:249
  467.0 31.9 %collective-permute-start.23 = (bf16[256,2048]{1,0:T(8,128)(2,1)}, bf16[256,2048]{1,0:T(8,128)(2,1)S(1)}, u32[]{:S(2)}, u32[]{:S(2)}) collective-permute-start(bf16[256,2048]{1,0:T(8,128)(2,1)} %add.213), channel_id=1, source_target_pairs={{1,2},{2,1},{5,6},{6,5},{9,10},{10,9},{13,14},{14,13},{17,18},{18,... | collective-permute-start | bytes 3145736 | tf_op jit(solution)/shard_map/ppermute | solution.py:188
  474.7 17.8 %copy-start.21 = (bf16[256,2048]{1,0:T(8,128)(2,1)S(1)}, bf16[256,2048]{1,0:T(8,128)(2,1)}, u32[]{:S(2)}) copy-start(bf16[256,2048]{1,0:T(8,128)(2,1)} %convolution_convert_fusion.16) | copy-start | bytes 3145732
  474.7 19.1 %copy-start.65 = (bf16[2048,1024]{0,1:T(8,128)(2,1)S(1)}, bf16[2048,1024]{0,1:T(8,128)(2,1)}, u32[]{:S(2)}) copy-start(bf16[2048,1024]{0,1:T(8,128)(2,1)} %copy-done.63) | copy-start | bytes 12582916
  476.8 41.3 %collective-permute-start.39 = (bf16[256,2048]{1,0:T(8,128)(2,1)S(1)}, bf16[256,2048]{1,0:T(8,128)(2,1)S(1)}, u32[]{:S(2)}, u32[]{:S(2)}) collective-permute-start(bf16[256,2048]{1,0:T(8,128)(2,1)S(1)} %add.225), channel_id=1, source_target_pairs={{1,0},{2,3},{5,4},{6,7},{9,8},{10,11},{13,12},{14,15},{17,16},{18,... | collective-permute-start | bytes 3145736 | tf_op jit(solution)/shard_map/ppermute | solution.py:188
  480.2 18.7 %copy-start.19 = (bf16[256,2048]{1,0:T(8,128)(2,1)S(1)}, bf16[256,2048]{1,0:T(8,128)(2,1)}, u32[]{:S(2)}) copy-start(bf16[256,2048]{1,0:T(8,128)(2,1)} %convolution_convert_fusion.7) | copy-start | bytes 3145732
  480.2 25.9 %collective-permute-start.22 = (bf16[256,2048]{1,0:T(8,128)(2,1)S(1)}, bf16[256,2048]{1,0:T(8,128)(2,1)S(1)}, u32[]{:S(2)}, u32[]{:S(2)}) collective-permute-start(bf16[256,2048]{1,0:T(8,128)(2,1)S(1)} %add.214), channel_id=1, source_target_pairs={{1,2},{2,1},{5,6},{6,5},{9,10},{10,9},{13,14},{14,13},{17,18},{18,... | collective-permute-start | bytes 3145736 | tf_op jit(solution)/shard_map/ppermute | solution.py:188
  481.1 34.9 %collective-permute-start.6 = (bf16[256,2048]{1,0:T(8,128)(2,1)S(1)}, bf16[256,2048]{1,0:T(8,128)(2,1)S(1)}, u32[]{:S(2)}, u32[]{:S(2)}) collective-permute-start(bf16[256,2048]{1,0:T(8,128)(2,1)S(1)} %copy-done.22), channel_id=1, source_target_pairs={{0,1},{3,2},{4,5},{7,6},{8,9},{11,10},{12,13},{15,14},{16,17},{19,... | collective-permute-start | bytes 3145736 | tf_op jit(solution)/shard_map/ppermute | solution.py:188
  492.5 46.0 %collective-permute-start.5 = (bf16[256,2048]{1,0:T(8,128)(2,1)S(1)}, bf16[256,2048]{1,0:T(8,128)(2,1)S(1)}, u32[]{:S(2)}, u32[]{:S(2)}) collective-permute-start(bf16[256,2048]{1,0:T(8,128)(2,1)S(1)} %copy-done.21), channel_id=1, source_target_pairs={{0,1},{3,2},{4,5},{7,6},{8,9},{11,10},{12,13},{15,14},{16,17},{19,... | collective-permute-start | bytes 3145736 | tf_op jit(solution)/shard_map/ppermute | solution.py:188
  498.8 60.2 %collective-permute-start.10 = (bf16[256,2048]{1,0:T(8,128)(2,1)S(1)}, bf16[256,2048]{1,0:T(8,128)(2,1)S(1)}, u32[]{:S(2)}, u32[]{:S(2)}) collective-permute-start(bf16[256,2048]{1,0:T(8,128)(2,1)S(1)} %copy-done.19), channel_id=1, source_target_pairs={{0,1},{3,2},{4,5},{7,6},{8,9},{11,10},{12,13},{15,14},{16,17},{19,... | collective-permute-start | bytes 3145736 | tf_op jit(solution)/shard_map/ppermute | solution.py:188
  506.1 54.2 %collective-permute-start.38 = (bf16[256,2048]{1,0:T(8,128)(2,1)S(1)}, bf16[256,2048]{1,0:T(8,128)(2,1)S(1)}, u32[]{:S(2)}, u32[]{:S(2)}) collective-permute-start(bf16[256,2048]{1,0:T(8,128)(2,1)S(1)} %add.226), channel_id=1, source_target_pairs={{1,0},{2,3},{5,4},{6,7},{9,8},{10,11},{13,12},{14,15},{17,16},{18,... | collective-permute-start | bytes 3145736 | tf_op jit(solution)/shard_map/ppermute | solution.py:188
  516.0 53.7 %collective-permute-start.37 = (bf16[256,2048]{1,0:T(8,128)(2,1)S(1)}, bf16[256,2048]{1,0:T(8,128)(2,1)S(1)}, u32[]{:S(2)}, u32[]{:S(2)}) collective-permute-start(bf16[256,2048]{1,0:T(8,128)(2,1)S(1)} %add.227), channel_id=1, source_target_pairs={{1,0},{2,3},{5,4},{6,7},{9,8},{10,11},{13,12},{14,15},{17,16},{18,... | collective-permute-start | bytes 3145736 | tf_op jit(solution)/shard_map/ppermute | solution.py:188
  518.1 72.0 %collective-permute-start.36 = (bf16[256,2048]{1,0:T(8,128)(2,1)S(1)}, bf16[256,2048]{1,0:T(8,128)(2,1)S(1)}, u32[]{:S(2)}, u32[]{:S(2)}) collective-permute-start(bf16[256,2048]{1,0:T(8,128)(2,1)S(1)} %add.228), channel_id=1, source_target_pairs={{1,0},{2,3},{5,4},{6,7},{9,8},{10,11},{13,12},{14,15},{17,16},{18,... | collective-permute-start | bytes 3145736 | tf_op jit(solution)/shard_map/ppermute | solution.py:188
  538.5 53.2 %collective-permute-start.21 = (bf16[256,2048]{1,0:T(8,128)(2,1)S(1)}, bf16[256,2048]{1,0:T(8,128)(2,1)S(1)}, u32[]{:S(2)}, u32[]{:S(2)}) collective-permute-start(bf16[256,2048]{1,0:T(8,128)(2,1)S(1)} %add.215), channel_id=1, source_target_pairs={{1,2},{2,1},{5,6},{6,5},{9,10},{10,9},{13,14},{14,13},{17,18},{18,... | collective-permute-start | bytes 3145736 | tf_op jit(solution)/shard_map/ppermute | solution.py:188
  540.5 29.1 %copy-start.20 = (bf16[256,2048]{1,0:T(8,128)(2,1)S(1)}, bf16[256,2048]{1,0:T(8,128)(2,1)}, u32[]{:S(2)}) copy-start(bf16[256,2048]{1,0:T(8,128)(2,1)} %convolution_convert_fusion.8) | copy-start | bytes 3145732
  559.0 34.5 %collective-permute-start.20 = (bf16[256,2048]{1,0:T(8,128)(2,1)S(1)}, bf16[256,2048]{1,0:T(8,128)(2,1)S(1)}, u32[]{:S(2)}, u32[]{:S(2)}) collective-permute-start(bf16[256,2048]{1,0:T(8,128)(2,1)S(1)} %add.216), channel_id=1, source_target_pairs={{1,2},{2,1},{5,6},{6,5},{9,10},{10,9},{13,14},{14,13},{17,18},{18,... | collective-permute-start | bytes 3145736 | tf_op jit(solution)/shard_map/ppermute | solution.py:188
  560.3 36.5 %collective-permute-start.19 = (bf16[256,2048]{1,0:T(8,128)(2,1)S(1)}, bf16[256,2048]{1,0:T(8,128)(2,1)S(1)}, u32[]{:S(2)}, u32[]{:S(2)}) collective-permute-start(bf16[256,2048]{1,0:T(8,128)(2,1)S(1)} %add.217), channel_id=1, source_target_pairs={{1,2},{2,1},{5,6},{6,5},{9,10},{10,9},{13,14},{14,13},{17,18},{18,... | collective-permute-start | bytes 3145736 | tf_op jit(solution)/shard_map/ppermute | solution.py:188
  569.7 28.9 %collective-permute-start.9 = (bf16[256,2048]{1,0:T(8,128)(2,1)S(1)}, bf16[256,2048]{1,0:T(8,128)(2,1)S(1)}, u32[]{:S(2)}, u32[]{:S(2)}) collective-permute-start(bf16[256,2048]{1,0:T(8,128)(2,1)S(1)} %copy-done.20), channel_id=1, source_target_pairs={{0,1},{3,2},{4,5},{7,6},{8,9},{11,10},{12,13},{15,14},{16,17},{19,... | collective-permute-start | bytes 3145736 | tf_op jit(solution)/shard_map/ppermute | solution.py:188
  590.1 25.0 %collective-permute-start.8 = (bf16[256,2048]{1,0:T(8,128)(2,1)S(1)}, bf16[256,2048]{1,0:T(8,128)(2,1)S(1)}, u32[]{:S(2)}, u32[]{:S(2)}) collective-permute-start(bf16[256,2048]{1,0:T(8,128)(2,1)S(1)} %convolution_convert_fusion.17), channel_id=1, source_target_pairs={{0,1},{3,2},{4,5},{7,6},{8,9},{11,10},{12,13},{15,14},{16,17},{19,... | collective-permute-start | bytes 3145736 | tf_op jit(solution)/shard_map/ppermute | solution.py:188
  591.6 43.3 %collective-permute-start.13 = (bf16[256,2048]{1,0:T(8,128)(2,1)S(1)}, bf16[256,2048]{1,0:T(8,128)(2,1)S(1)}, u32[]{:S(2)}, u32[]{:S(2)}) collective-permute-start(bf16[256,2048]{1,0:T(8,128)(2,1)S(1)} %convolution_convert_fusion.6), channel_id=1, source_target_pairs={{0,1},{3,2},{4,5},{7,6},{8,9},{11,10},{12,13},{15,14},{16,17},{19,... | collective-permute-start | bytes 3145736 | tf_op jit(solution)/shard_map/ppermute | solution.py:188
  593.6 48.6 %collective-permute-start.35 = (bf16[256,2048]{1,0:T(8,128)(2,1)S(1)}, bf16[256,2048]{1,0:T(8,128)(2,1)S(1)}, u32[]{:S(2)}, u32[]{:S(2)}) collective-permute-start(bf16[256,2048]{1,0:T(8,128)(2,1)S(1)} %add.229), channel_id=1, source_target_pairs={{1,0},{2,3},{5,4},{6,7},{9,8},{10,11},{13,12},{14,15},{17,16},{18,... | collective-permute-start | bytes 3145736 | tf_op jit(solution)/shard_map/ppermute | solution.py:188
  596.8 52.5 %collective-permute-start.34 = (bf16[256,2048]{1,0:T(8,128)(2,1)S(1)}, bf16[256,2048]{1,0:T(8,128)(2,1)S(1)}, u32[]{:S(2)}, u32[]{:S(2)}) collective-permute-start(bf16[256,2048]{1,0:T(8,128)(2,1)S(1)} %add.230), channel_id=1, source_target_pairs={{1,0},{2,3},{5,4},{6,7},{9,8},{10,11},{13,12},{14,15},{17,16},{18,... | collective-permute-start | bytes 3145736 | tf_op jit(solution)/shard_map/ppermute | solution.py:188
  598.5 66.2 %collective-permute-start.33 = (bf16[256,2048]{1,0:T(8,128)(2,1)S(1)}, bf16[256,2048]{1,0:T(8,128)(2,1)S(1)}, u32[]{:S(2)}, u32[]{:S(2)}) collective-permute-start(bf16[256,2048]{1,0:T(8,128)(2,1)S(1)} %add.231), channel_id=1, source_target_pairs={{1,0},{2,3},{5,4},{6,7},{9,8},{10,11},{13,12},{14,15},{17,16},{18,... | collective-permute-start | bytes 3145736 | tf_op jit(solution)/shard_map/ppermute | solution.py:188
  615.2 45.5 %collective-permute-start.18 = (bf16[256,2048]{1,0:T(8,128)(2,1)S(1)}, bf16[256,2048]{1,0:T(8,128)(2,1)S(1)}, u32[]{:S(2)}, u32[]{:S(2)}) collective-permute-start(bf16[256,2048]{1,0:T(8,128)(2,1)S(1)} %add.218), channel_id=1, source_target_pairs={{1,2},{2,1},{5,6},{6,5},{9,10},{10,9},{13,14},{14,13},{17,18},{18,... | collective-permute-start | bytes 3145736 | tf_op jit(solution)/shard_map/ppermute | solution.py:188
  615.9 27.0 %slice-start = ((s8[8388608]{0:T(1024)(128)(4,1)}), s8[4194304]{0:T(1024)(128)(4,1)S(1)}, s32[]{:S(2)}) async-start(s8[8388608]{0:T(1024)(128)(4,1)} %bitcast.107), calls=%async_computation.13 | async-start | bytes 8388608
  634.9 29.8 %collective-permute-start.17 = (bf16[256,2048]{1,0:T(8,128)(2,1)S(1)}, bf16[256,2048]{1,0:T(8,128)(2,1)S(1)}, u32[]{:S(2)}, u32[]{:S(2)}) collective-permute-start(bf16[256,2048]{1,0:T(8,128)(2,1)S(1)} %add.219), channel_id=1, source_target_pairs={{1,2},{2,1},{5,6},{6,5},{9,10},{10,9},{13,14},{14,13},{17,18},{18,... | collective-permute-start | bytes 3145736 | tf_op jit(solution)/shard_map/ppermute | solution.py:188
  642.1 25.3 %collective-permute-start.16 = (bf16[256,2048]{1,0:T(8,128)(2,1)S(1)}, bf16[256,2048]{1,0:T(8,128)(2,1)S(1)}, u32[]{:S(2)}, u32[]{:S(2)}) collective-permute-start(bf16[256,2048]{1,0:T(8,128)(2,1)S(1)} %add.220), channel_id=1, source_target_pairs={{1,2},{2,1},{5,6},{6,5},{9,10},{10,9},{13,14},{14,13},{17,18},{18,... | collective-permute-start | bytes 3145736 | tf_op jit(solution)/shard_map/ppermute | solution.py:188
  649.3 52.1 %collective-permute-start.11 = (bf16[2048,384]{1,0:T(8,128)(2,1)}, bf16[2048,384]{1,0:T(8,128)(2,1)}, u32[]{:S(2)}, u32[]{:S(2)}) collective-permute-start(bf16[2048,384]{1,0:T(8,128)(2,1)} %convolution_convert_fusion.4), channel_id=1, source_target_pairs={{0,1},{3,2},{4,5},{7,6},{8,9},{11,10},{12,13},{15,14},{16,17},{19,... | collective-permute-start | bytes 4718600 | tf_op jit(solution)/shard_map/ppermute | solution.py:188
  662.0 30.6 %collective-permute-start.32 = (bf16[256,2048]{1,0:T(8,128)(2,1)}, bf16[256,2048]{1,0:T(8,128)(2,1)}, u32[]{:S(2)}, u32[]{:S(2)}) collective-permute-start(bf16[256,2048]{1,0:T(8,128)(2,1)} %add.232), channel_id=1, source_target_pairs={{1,0},{2,3},{5,4},{6,7},{9,8},{10,11},{13,12},{14,15},{17,16},{18,... | collective-permute-start | bytes 3145736 | tf_op jit(solution)/shard_map/ppermute | solution.py:188
  666.1 46.7 %collective-permute-start.31 = (bf16[256,2048]{1,0:T(8,128)(2,1)}, bf16[256,2048]{1,0:T(8,128)(2,1)}, u32[]{:S(2)}, u32[]{:S(2)}) collective-permute-start(bf16[256,2048]{1,0:T(8,128)(2,1)} %add.233), channel_id=1, source_target_pairs={{1,0},{2,3},{5,4},{6,7},{9,8},{10,11},{13,12},{14,15},{17,16},{18,... | collective-permute-start | bytes 3145736 | tf_op jit(solution)/shard_map/ppermute | solution.py:188
  668.8 62.1 %collective-permute-start.30 = (bf16[256,2048]{1,0:T(8,128)(2,1)}, bf16[256,2048]{1,0:T(8,128)(2,1)}, u32[]{:S(2)}, u32[]{:S(2)}) collective-permute-start(bf16[256,2048]{1,0:T(8,128)(2,1)} %add.234), channel_id=1, source_target_pairs={{1,0},{2,3},{5,4},{6,7},{9,8},{10,11},{13,12},{14,15},{17,16},{18,... | collective-permute-start | bytes 3145736 | tf_op jit(solution)/shard_map/ppermute | solution.py:188
  670.1 30.2 %collective-permute-start.12 = (bf16[128,2048]{1,0:T(8,128)(2,1)}, bf16[128,2048]{1,0:T(8,128)(2,1)S(1)}, u32[]{:S(2)}, u32[]{:S(2)}) collective-permute-start(bf16[128,2048]{1,0:T(8,128)(2,1)} %reduce-scatter.11.cloned.1.call-done), channel_id=1, source_target_pairs={{0,1},{3,2},{4,5},{7,6},{8,9},{11,10},{12,13},{15,14},{16,17},{19,... | collective-permute-start | bytes 1572872 | tf_op jit(solution)/shard_map/ppermute | solution.py:188
  703.8 31.9 %collective-permute-start.14 = (bf16[2048,384]{1,0:T(8,128)(2,1)S(1)}, bf16[2048,384]{1,0:T(8,128)(2,1)S(1)}, u32[]{:S(2)}, u32[]{:S(2)}) collective-permute-start(bf16[2048,384]{1,0:T(8,128)(2,1)S(1)} %add.222), channel_id=1, source_target_pairs={{1,2},{2,1},{5,6},{6,5},{9,10},{10,9},{13,14},{14,13},{17,18},{18,... | collective-permute-start | bytes 4718600 | tf_op jit(solution)/shard_map/ppermute | solution.py:188
  730.9 3.3 collective-permute-start.15
  734.4 33.4 %collective-permute-start.29 = (bf16[128,2048]{1,0:T(8,128)(2,1)S(1)}, bf16[128,2048]{1,0:T(8,128)(2,1)S(1)}, u32[]{:S(2)}, u32[]{:S(2)}) collective-permute-start(bf16[128,2048]{1,0:T(8,128)(2,1)S(1)} %add.235), channel_id=1, source_target_pairs={{1,0},{2,3},{5,4},{6,7},{9,8},{10,11},{13,12},{14,15},{17,16},{18,... | collective-permute-start | bytes 1572872 | tf_op jit(solution)/shard_map/ppermute | solution.py:188
  737.2 60.6 %collective-permute-start.28 = (bf16[2048,384]{1,0:T(8,128)(2,1)}, bf16[2048,384]{1,0:T(8,128)(2,1)}, u32[]{:S(2)}, u32[]{:S(2)}) collective-permute-start(bf16[2048,384]{1,0:T(8,128)(2,1)} %add.236), channel_id=1, source_target_pairs={{1,0},{2,3},{5,4},{6,7},{9,8},{10,11},{13,12},{14,15},{17,16},{18,... | collective-permute-start | bytes 4718600 | tf_op jit(solution)/shard_map/ppermute | solution.py:188
  (60 other events, 250.7 us)
Sparse Core Ops, SparseCore 0:
  9.9 57.0 all-gather.4
  68.9 36.7 all-gather.8
  108.1 37.4 all-gather.6
  147.3 54.3 all-gather.10
  249.7 71.2 reduce-scatter.6
  325.2 71.2 reduce-scatter.4
  444.8 55.6 reduce-scatter.10
  504.3 71.2 reduce-scatter.8
where the time goes:
time: 862 us; the launch traced here: 853 us
  waiting for transfers between devices  344 us (40%)
  matrix products  207 us (24%)
  starting transfers between devices  109 us (13%)
  other arithmetic  95.5 us (11%)
  local copies, waits for them, and re-layouts  41.4 us (5%)
  blocking collectives  38.3 us (4%)
  between operations  17.7 us (2%)
    ppermute x42, waiting for transfers between devices, add(): arrived = lax.ppermute(array, self.axis, pairs)  182 us
    ppermute x42, starting transfers between devices, add(): arrived = lax.ppermute(array, self.axis, pairs)  104 us
    dot_general x14, matrix products, dot_cols(): lax.dot_general(left_mat, right_mat, (((0,), (0,)), ((), ())), preferred_...  78.3 us
    all_gather x3, waiting for transfers between devices, gather(): return lax.all_gather(array, 'heads', axis=0, tiled=True)  64.1 us
    reduce_scatter x4, waiting for transfers between devices, scatter(): return lax.psum_scatter(array, 'heads', scatter_dimension=0, tiled=True)  56.7 us
    dot_general x4, matrix products, dot_rows(): lax.dot_general(left_mat, right_mat, (((1,), (1,)), ((), ())), preferred_...  53.9 us
    all_gather x1, waiting for transfers between devices, per_device(): mixed_all = lax.all_gather(mixed, 'heads', axis=1, tiled=True)  39.9 us
    psum x1, blocking collectives, per_device(): lax.psum(jnp.concatenate([gain_attn_part, gain_mlp_part, slots]), ('heads...  38.3 us
  transfers between devices with their start and end apart: 51, of which 17 were waited for; matrix products, arithmetic and copies ran while one was open for 33% of the time, Pallas kernels for 0%

commit v1 on v0

--- a/solution.py
+++ b/solution.py
@@ -10,6 +10,12 @@
 MICRO = 2
 epsilon = 1e-05
 big_negative = -1e30
+
+
+def in_order(blocks, dim):
+    shape = list(blocks.shape[1:])
+    shape[dim] *= blocks.shape[0]
+    return jnp.moveaxis(blocks, 0, dim).reshape(shape)
 
 
 def dot_rows(left_mat, right_mat):
@@ -268,7 +274,19 @@
     query, key, value = [by_sequence(qkv[:, i * DH : (i + 1) * DH]) for i in range(3)]
     head_kept = head_forward(query, key, value, share, positions, doc_ids, valid_keys)
     mixed = by_device(head_kept[0].astype(low))
-    mixed_all = lax.all_gather(mixed, "heads", axis=1, tiled=True)
+    count = lax.axis_size("heads")
+    pairs_2 = [(i_2, (i_2 + 1) % count) for i_2 in range(count)]
+    back = [(b, a) for a, b in pairs_2]
+    lower, upper = ([], [])
+    for hop in range(count - 1):
+        if hop % 2 == 0:
+            lower.append(lax.ppermute(lower[-1] if lower else mixed, "heads", pairs_2))
+        else:
+            upper.append(lax.ppermute(upper[-1] if upper else mixed, "heads", back))
+    blocks = jnp.stack([*lower[::-1], mixed, *upper])
+    shift = lax.axis_index("heads") - len(lower)
+    blocks = blocks[(jnp.arange(count) - shift) % count]
+    mixed_all = in_order(blocks, 1)
     cot_all = gather(cot_own)
     y1_all = x_all + jnp.dot(mixed_all, w_out_all, preferred_element_type=jnp.float32)
     h2_all = (y1_all * norm_scale(y1_all) * norm_mlp).astype(low)

time: 862 us -> 901 us (1.045)
  local copies, waits for them, and re-layouts: 41.4 us -> 56.7 us
  waiting for transfers between devices: 344 us -> 359 us
    ppermute x0 -> x7, waiting for transfers between devices: none -> 66.2 us  [the longest x4 66.2 us: per_device(): lower.append(lax.ppermute(lower[-1] if lower else mixed, 'heads', pairs_2))]
    all_gather x1 -> x0, waiting for transfers between devices: 39.9 us -> none  [per_device(): mixed_all = lax.all_gather(mixed, 'heads', axis=1, tiled=True)]
    all_gather x3, waiting for transfers between devices: 64.1 us -> 52.2 us  [gather(): return lax.all_gather(array, 'heads', axis=0, tiled=True)]
    unnamed x150 -> x161, local copies, waits for them, and re-layouts: 20.8 us -> 26.1 us
  transfers between devices with their start and end apart: 51 -> 57, of which waited for: 17 -> 18; matrix products, arithmetic and copies ran while one was open for 33% -> 33% of each run, Pallas kernels for 0% -> 0%
where the time goes in v1:
time: 901 us; the launch traced here: 892 us
  waiting for transfers between devices  359 us (40%)
  matrix products  208 us (23%)
  starting transfers between devices  117 us (13%)
  other arithmetic  95.4 us (11%)
  local copies, waits for them, and re-layouts  56.7 us (6%)
  blocking collectives  38.6 us (4%)
  between operations  17.8 us (2%)
    ppermute x42, waiting for transfers between devices, add(): arrived = lax.ppermute(array, self.axis, pairs)  182 us
    ppermute x42, starting transfers between devices, add(): arrived = lax.ppermute(array, self.axis, pairs)  104 us
    dot_general x14, matrix products, dot_cols(): lax.dot_general(left_mat, right_mat, (((0,), (0,)), ((), ())), preferred_...  77.9 us
    ppermute x4, waiting for transfers between devices, per_device(): lower.append(lax.ppermute(lower[-1] if lower else mixed, 'heads', pairs_2))  66.2 us
    reduce_scatter x4, waiting for transfers between devices, scatter(): return lax.psum_scatter(array, 'heads', scatter_dimension=0, tiled=True)  56.4 us
    dot_general x4, matrix products, dot_rows(): lax.dot_general(left_mat, right_mat, (((1,), (1,)), ((), ())), preferred_...  53.8 us
    all_gather x3, waiting for transfers between devices, gather(): return lax.all_gather(array, 'heads', axis=0, tiled=True)  52.2 us
    psum x1, blocking collectives, per_device(): lax.psum(jnp.concatenate([gain_attn_part, gain_mlp_part, slots]), ('heads...  38.6 us
  transfers between devices with their start and end apart: 57, of which 18 were waited for; matrix products, arithmetic and copies ran while one was open for 33% of the time, Pallas kernels for 0%

profile of v1, /device:TPU:0, one launch (start us, length us, event | category | flops | bytes accessed | tf_op | source)
XLA Modules:
  0.0 891.8 jit_solution(17749934055492586856)
XLA Ops:
  14.9 52.2 %all-gather.4.cloned.1.call-done = bf16[2048,2048]{1,0:T(8,128)(2,1)} async-done(((bf16[256,2048]{1,0:T(8,128)(2,1)}), bf16[2048,2048]{1,0:T(8,128)(2,1)}) %all-gather.4.cloned.1.call-update) | async-done | bytes 8388624 | tf_op jit(solution)/shard_map/all_gather | solution.py:252
  67.0 5.2 fusion.2
  72.8 4.8 convolution_convert_fusion.5
  86.6 3.8 broadcast_divide_fusion.2
  92.2 18.3 %collective-permute-done = bf16[2048,128]{1,0:T(8,128)(2,1)S(1)} collective-permute-done((bf16[2048,128]{1,0:T(8,128)(2,1)S(1)}, bf16[2048,128]{1,0:T(8,128)(2,1)S(1)}, u32[]{:S(2)}, u32[]{:S(2)}) %collective-permute-start) | collective-permute-done | bytes 524320 | tf_op jit(solution)/shard_map/ppermute | solution.py:283
  113.1 14.4 %collective-permute-done.1 = bf16[2048,128]{1,0:T(8,128)(2,1)S(1)} collective-permute-done((bf16[2048,128]{1,0:T(8,128)(2,1)S(1)}, bf16[2048,128]{1,0:T(8,128)(2,1)S(1)}, u32[]{:S(2)}, u32[]{:S(2)}) %collective-permute-start.1) | collective-permute-done | bytes 524320 | tf_op jit(solution)/shard_map/ppermute | solution.py:283
  127.5 2.8 constant_dynamic-update-slice_fusion.5
  133.1 14.9 %collective-permute-done.2 = bf16[2048,128]{1,0:T(8,128)(2,1)S(1)} collective-permute-done((bf16[2048,128]{1,0:T(8,128)(2,1)S(1)}, bf16[2048,128]{1,0:T(8,128)(2,1)S(1)}, u32[]{:S(2)}, u32[]{:S(2)}) %collective-permute-start.2) | collective-permute-done | bytes 524320 | tf_op jit(solution)/shard_map/ppermute | solution.py:283
  148.7 3.4 copy-done.14
  154.7 18.6 %collective-permute-done.3 = bf16[2048,128]{1,0:T(8,128)(2,1)S(1)} collective-permute-done((bf16[2048,128]{1,0:T(8,128)(2,1)S(1)}, bf16[2048,128]{1,0:T(8,128)(2,1)S(1)}, u32[]{:S(2)}, u32[]{:S(2)}) %collective-permute-start.3) | collective-permute-done | bytes 524320 | tf_op jit(solution)/shard_map/ppermute | solution.py:283
  179.9 5.3 gather_fusion
  185.2 6.7 copy.64
  191.9 14.8 %multiply_reduce_fusion = (f32[2048]{0:T(1024)S(1)}, f32[2048,2048]{1,0:T(8,128)S(1)}) fusion(bf16[2048,1024]{0,1:T(8,128)(2,1)} %bitcast.135, bf16[1024,2048]{1,0:T(8,128)(2,1)} %all-gather.6.cloned.1.call-done, bf16[2048,2048]{1,0:T(8,128)(2,1)} %all-gather.4.cloned.1.call-done), kind=kOutput, calls=%fused_computation.10 | convolution fusion | flops 8606709760 | bytes 33562624 | tf_op jit(solution)/shard_map/dot_general | solution.py:291
  206.8 5.8 copy-done
  212.6 4.4 multiply_convert_fusion
  217.0 24.3 %fusion.127 = f32[2048,2048]{0,1:T(8,128)} fusion(bf16[2048,2048]{1,0:T(8,128)(2,1)} %multiply_convert_fusion, bf16[2048,2048]{1,0:T(8,128)(2,1)} %copy-done.14), kind=kOutput, calls=%fused_computation.239 | convolution fusion | flops 17179869184 | bytes 33554432 | tf_op jit(solution)/shard_map/dot_general | solution.py:295
  241.3 22.8 %multiply_convert_fusion.2 = (bf16[2048,1024]{0,1:T(8,128)(2,1)S(1)}, bf16[2048,1024]{0,1:T(8,128)(2,1)}, bf16[2048,1024]{0,1:T(8,128)(2,1)}) fusion(f32[2048,2048]{0,1:T(8,128)} %fusion.127, bf16[2048,2048]{1,0:T(8,128)(2,1)} %all-gather.8.cloned.1.call-done, bf16[1024,2048]{1,0:T(8,128)(2,1)} %param.24), kind=kOutput, calls=%fused_computation.13 | convolution fusion | flops 8623489024 | bytes 41943040 | tf_op jit(solution)/shard_map/dot_general | solution.py:22
  266.1 22.9 %convolution_convert_fusion.1 = bf16[2048,2048]{1,0:T(8,128)(2,1)} fusion(bf16[2048,2048]{1,0:T(8,128)(2,1)} %copy-done.14, bf16[2048,1024]{0,1:T(8,128)(2,1)} %get-tuple-element.249, bf16[2048,1024]{0,1:T(8,128)(2,1)S(1)} %get-tuple-element.248), kind=kOutput, calls=%fused_computation.17 | convolution fusion | flops 17200840704 | bytes 25165824 | tf_op jit(solution)/shard_map/dot_general | solution.py:22
  289.1 14.5 %convolution_convert_fusion.2 = bf16[2048,2048]{1,0:T(8,128)(2,1)} fusion(bf16[2048,1024]{0,1:T(8,128)(2,1)} %get-tuple-element.252, bf16[1024,2048]{1,0:T(8,128)(2,1)} %param.24), kind=kOutput, calls=%fused_computation.18 | convolution fusion | flops 8594128896 | bytes 16777216 | tf_op jit(solution)/shard_map/dot_general | solution.py:315
  305.7 6.2 convolution_convert_fusion.13
  311.9 4.0 collective-permute-start.8
  315.9 6.4 convolution_convert_fusion.14
  324.4 3.4 convolution_convert_fusion.15
  327.8 3.4 convolution_convert_fusion.9
  331.2 5.7 convolution_convert_fusion.10
  337.0 7.1 convolution_convert_fusion.16
  344.1 4.9 convolution_convert_fusion.11
  348.9 7.2 convolution_convert_fusion.7
  360.3 4.5 convolution_convert_fusion.12
  370.0 3.3 collective-permute-start.10
  375.6 3.1 fusion.16
  378.8 56.3 %reduce-scatter.5.cloned.1.call-done = bf16[256,2048]{1,0:T(8,128)(2,1)} async-done(((bf16[2048,2048]{1,0:T(8,128)(2,1)}), bf16[256,2048]{1,0:T(8,128)(2,1)}) %reduce-scatter.5.cloned.1.call-update) | async-done | bytes 1048592 | tf_op jit(solution)/shard_map/reduce_scatter | solution.py:255
  435.1 4.6 fusion.13
  441.9 4.2 all-to-all-start
  446.1 7.1 convolution_convert_fusion.8
  453.2 2.9 add.237
  457.8 6.1 collective-permute-start.14
  468.3 2.9 add.250
  476.1 2.9 add.239
  479.0 4.3 convolution_convert_fusion.3
  498.7 6.8 convolution_convert_fusion
  506.5 6.3 convolution_convert_fusion.17
  519.2 11.7 %collective-permute-start.13 = (bf16[256,2048]{1,0:T(8,128)(2,1)S(1)}, bf16[256,2048]{1,0:T(8,128)(2,1)S(1)}, u32[]{:S(2)}, u32[]{:S(2)}) collective-permute-start(bf16[256,2048]{1,0:T(8,128)(2,1)S(1)} %copy-done.24), channel_id=1, source_target_pairs={{0,1},{3,2},{4,5},{7,6},{8,9},{11,10},{12,13},{15,14},{16,17},{19,... | collective-permute-start | bytes 3145736 | tf_op jit(solution)/shard_map/ppermute | solution.py:194
  532.3 5.0 convolution_convert_fusion.6
  537.3 3.7 collective-permute-start.17
  545.6 8.8 collective-permute-done.13
  557.8 19.1 %collective-permute-done.12 = bf16[256,2048]{1,0:T(8,128)(2,1)S(1)} collective-permute-done((bf16[256,2048]{1,0:T(8,128)(2,1)S(1)}, bf16[256,2048]{1,0:T(8,128)(2,1)S(1)}, u32[]{:S(2)}, u32[]{:S(2)}) %collective-permute-start.12) | collective-permute-done | bytes 1048608 | tf_op jit(solution)/shard_map/ppermute | solution.py:194
  579.4 18.0 %collective-permute-done.17 = bf16[256,2048]{1,0:T(8,128)(2,1)S(1)} collective-permute-done((bf16[256,2048]{1,0:T(8,128)(2,1)S(1)}, bf16[256,2048]{1,0:T(8,128)(2,1)S(1)}, u32[]{:S(2)}, u32[]{:S(2)}) %collective-permute-start.17) | collective-permute-done | bytes 1048608 | tf_op jit(solution)/shard_map/ppermute | solution.py:194
  599.4 8.5 collective-permute-done.44
  609.4 18.9 %collective-permute-done.43 = bf16[256,2048]{1,0:T(8,128)(2,1)S(1)} collective-permute-done((bf16[256,2048]{1,0:T(8,128)(2,1)S(1)}, bf16[256,2048]{1,0:T(8,128)(2,1)S(1)}, u32[]{:S(2)}, u32[]{:S(2)}) %collective-permute-start.43) | collective-permute-done | bytes 1048608 | tf_op jit(solution)/shard_map/ppermute | solution.py:194
  638.4 14.9 %collective-permute-done.15 = bf16[256,2048]{1,0:T(8,128)(2,1)S(1)} collective-permute-done((bf16[256,2048]{1,0:T(8,128)(2,1)S(1)}, bf16[256,2048]{1,0:T(8,128)(2,1)S(1)}, u32[]{:S(2)}, u32[]{:S(2)}) %collective-permute-start.15) | collective-permute-done | bytes 1048608 | tf_op jit(solution)/shard_map/ppermute | solution.py:194
  654.5 18.7 %collective-permute-done.20 = bf16[256,2048]{1,0:T(8,128)(2,1)S(1)} collective-permute-done((bf16[256,2048]{1,0:T(8,128)(2,1)S(1)}, bf16[256,2048]{1,0:T(8,128)(2,1)S(1)}, u32[]{:S(2)}, u32[]{:S(2)}) %collective-permute-start.20) | collective-permute-done | bytes 1048608 | tf_op jit(solution)/shard_map/ppermute | solution.py:194
  674.4 4.6 maximum_convert_fusion
  681.2 6.4 convolution_convert_fusion.4
  687.6 10.0 %collective-permute-start.18 = (bf16[2048,384]{1,0:T(8,128)(2,1)}, bf16[2048,384]{1,0:T(8,128)(2,1)}, u32[]{:S(2)}, u32[]{:S(2)}) collective-permute-start(bf16[2048,384]{1,0:T(8,128)(2,1)} %convolution_convert_fusion.4), channel_id=1, source_target_pairs={{0,1},{3,2},{4,5},{7,6},{8,9},{11,10},{12,13},{15,14},{16,17},{19,... | collective-permute-start | bytes 4718600 | tf_op jit(solution)/shard_map/ppermute | solution.py:194
  708.4 20.1 %collective-permute-start.19 = (bf16[128,2048]{1,0:T(8,128)(2,1)}, bf16[128,2048]{1,0:T(8,128)(2,1)S(1)}, u32[]{:S(2)}, u32[]{:S(2)}) collective-permute-start(bf16[128,2048]{1,0:T(8,128)(2,1)} %reduce-scatter.11.cloned.1.call-done), channel_id=1, source_target_pairs={{0,1},{3,2},{4,5},{7,6},{8,9},{11,10},{12,13},{15,14},{16,17},{19,... | collective-permute-start | bytes 1572872 | tf_op jit(solution)/shard_map/ppermute | solution.py:194
  731.1 7.6 collective-permute-done.19
  745.5 5.6 collective-permute-done.38
  753.7 15.5 %collective-permute-done.37 = bf16[256,2048]{1,0:T(8,128)(2,1)} collective-permute-done((bf16[256,2048]{1,0:T(8,128)(2,1)}, bf16[256,2048]{1,0:T(8,128)(2,1)}, u32[]{:S(2)}, u32[]{:S(2)}) %collective-permute-start.37) | collective-permute-done | bytes 1048608 | tf_op jit(solution)/shard_map/ppermute | solution.py:194
  776.8 11.8 %fusion.111 = (f32[2048,1024]{1,0:T(8,128)}, f32[2048,1024]{1,0:T(8,128)}) fusion(bf16[2048,2048]{1,0:T(8,128)(2,1)} %constant_dynamic-update-slice_fusion.6), kind=kLoop, calls=%fused_computation.231 | loop fusion | bytes 33554432 | tf_op jit(solution)/shard_map/slice | solution.py:348
  789.1 17.0 %collective-permute-done.36 = bf16[128,2048]{1,0:T(8,128)(2,1)S(1)} collective-permute-done((bf16[128,2048]{1,0:T(8,128)(2,1)S(1)}, bf16[128,2048]{1,0:T(8,128)(2,1)S(1)}, u32[]{:S(2)}, u32[]{:S(2)}) %collective-permute-start.36) | collective-permute-done | bytes 524320 | tf_op jit(solution)/shard_map/ppermute | solution.py:194
  807.2 29.0 %collective-permute-done.35 = bf16[2048,384]{1,0:T(8,128)(2,1)} collective-permute-done((bf16[2048,384]{1,0:T(8,128)(2,1)}, bf16[2048,384]{1,0:T(8,128)(2,1)}, u32[]{:S(2)}, u32[]{:S(2)}) %collective-permute-start.35) | collective-permute-done | bytes 1572896 | tf_op jit(solution)/shard_map/ppermute | solution.py:194
  841.5 38.6 %psum.7 = f32[4104]{0:T(1024)S(1)} all-reduce(f32[4104]{0:T(1024)S(1)} %pad_maximum_fusion.6), channel_id=1, replica_groups=mesh['heads'=8,'batch'=4] {'heads','batch'}, use_global_device_ids=true, to_apply=%region_23.24 | all-reduce | flops 4104 | bytes 32832 | tf_op jit(solution)/shard_map/psum | solution.py:334
  881.2 3.3 fusion.11
  (371 shorter events, 153.6 us)
Async XLA Ops:
  7.2 59.8 %all-gather.4.cloned.1.call-start = ((), (), s32[]{:S(2)}) async-start(), calls=%async_computation.5 | async-start | bytes 9437184 | tf_op jit(solution)/shard_map/all_gather | solution.py:252
  7.9 184.0 %all-gather.6.cloned.1.call-start = ((), (), s32[]{:S(2)}) async-start(), calls=%async_computation.6 | async-start | bytes 4718592 | tf_op jit(solution)/shard_map/all_gather | solution.py:252
  8.7 232.6 %all-gather.8.cloned.1.call-start = ((), (), s32[]{:S(2)}) async-start(), calls=%async_computation.8 | async-start | bytes 9437184 | tf_op jit(solution)/shard_map/all_gather | solution.py:252
  9.4 366.2 %reduce-scatter.7.cloned.1.call-start = ((), (), s32[]{:S(2)}) async-start(), calls=%async_computation.9 | async-start | bytes 9437184 | tf_op jit(solution)/shard_map/reduce_scatter | solution.py:255
  11.6 75.0 %copy-start.57 = (s32[2,512]{1,0:T(2,128)}, s32[2,512]{1,0:T(2,128)S(1)}, u32[]{:S(2)}) copy-start(s32[2,512]{1,0:T(2,128)S(1)} %get-tuple-element.265) | copy-start | bytes 12292
  11.6 75.0 %copy-start.59 = (s32[2,512]{1,0:T(2,128)}, s32[2,512]{1,0:T(2,128)S(1)}, u32[]{:S(2)}) copy-start(s32[2,512]{1,0:T(2,128)S(1)} %get-tuple-element.266) | copy-start | bytes 12292
  12.3 74.2 %copy-start.61 = (pred[2,512]{1,0:T(4,128)(4,1)}, pred[2,512]{1,0:T(4,128)(4,1)S(1)}, u32[]{:S(2)}) copy-start(pred[2,512]{1,0:T(4,128)(4,1)S(1)} %get-tuple-element.268) | copy-start | bytes 3076
  14.8 57.5 %copy-start.40 = (bf16[2048,384]{1,0:T(8,128)(2,1)}, bf16[2048,384]{1,0:T(8,128)(2,1)S(1)}, u32[]{:S(2)}) copy-start(bf16[2048,384]{1,0:T(8,128)(2,1)S(1)} %constant_dynamic-update-slice_fusion) | copy-start | bytes 4718596
  14.8 57.5 %copy-start.44 = (f32[2048]{0:T(1024)S(1)}, f32[2048]{0:T(1024)}, u32[]{:S(2)}) copy-start(f32[2048]{0:T(1024)} %param.25) | copy-start | bytes 24580
  91.9 18.6 %collective-permute-start = (bf16[2048,128]{1,0:T(8,128)(2,1)S(1)}, bf16[2048,128]{1,0:T(8,128)(2,1)S(1)}, u32[]{:S(2)}, u32[]{:S(2)}) collective-permute-start(bf16[2048,128]{1,0:T(8,128)(2,1)S(1)} %bitcast.142), channel_id=1, source_target_pairs={{0,4},{4,8},{8,12},{12,16},{16,20},{20,24},{24,28},{28,0},{1,5},{5... | collective-permute-start | bytes 1572872 | tf_op jit(solution)/shard_map/ppermute | solution.py:283
  110.5 17.0 %collective-permute-start.1 = (bf16[2048,128]{1,0:T(8,128)(2,1)S(1)}, bf16[2048,128]{1,0:T(8,128)(2,1)S(1)}, u32[]{:S(2)}, u32[]{:S(2)}) collective-permute-start(bf16[2048,128]{1,0:T(8,128)(2,1)S(1)} %collective-permute-done), channel_id=1, source_target_pairs={{0,4},{4,8},{8,12},{12,16},{16,20},{20,24},{24,28},{28,0},{1,5},{5... | collective-permute-start | bytes 1572872 | tf_op jit(solution)/shard_map/ppermute | solution.py:283
  110.5 19.9 %collective-permute-start.4 = (bf16[2048,128]{1,0:T(8,128)(2,1)S(1)}, bf16[2048,128]{1,0:T(8,128)(2,1)S(1)}, u32[]{:S(2)}, u32[]{:S(2)}) collective-permute-start(bf16[2048,128]{1,0:T(8,128)(2,1)S(1)} %bitcast.143), channel_id=1, source_target_pairs={{4,0},{8,4},{12,8},{16,12},{20,16},{24,20},{28,24},{0,28},{5,1},{9... | collective-permute-start | bytes 1572872 | tf_op jit(solution)/shard_map/ppermute | solution.py:285
  127.5 20.4 %collective-permute-start.2 = (bf16[2048,128]{1,0:T(8,128)(2,1)S(1)}, bf16[2048,128]{1,0:T(8,128)(2,1)S(1)}, u32[]{:S(2)}, u32[]{:S(2)}) collective-permute-start(bf16[2048,128]{1,0:T(8,128)(2,1)S(1)} %collective-permute-done.1), channel_id=1, source_target_pairs={{0,4},{4,8},{8,12},{12,16},{16,20},{20,24},{24,28},{28,0},{1,5},{5... | collective-permute-start | bytes 1572872 | tf_op jit(solution)/shard_map/ppermute | solution.py:283
  130.4 21.7 %collective-permute-start.5 = (bf16[2048,128]{1,0:T(8,128)(2,1)S(1)}, bf16[2048,128]{1,0:T(8,128)(2,1)S(1)}, u32[]{:S(2)}, u32[]{:S(2)}) collective-permute-start(bf16[2048,128]{1,0:T(8,128)(2,1)S(1)} %collective-permute-done.4), channel_id=1, source_target_pairs={{4,0},{8,4},{12,8},{16,12},{20,16},{24,20},{28,24},{0,28},{5,1},{9... | collective-permute-start | bytes 1572872 | tf_op jit(solution)/shard_map/ppermute | solution.py:285
  148.0 25.3 %collective-permute-start.3 = (bf16[2048,128]{1,0:T(8,128)(2,1)S(1)}, bf16[2048,128]{1,0:T(8,128)(2,1)S(1)}, u32[]{:S(2)}, u32[]{:S(2)}) collective-permute-start(bf16[2048,128]{1,0:T(8,128)(2,1)S(1)} %collective-permute-done.2), channel_id=1, source_target_pairs={{0,4},{4,8},{8,12},{12,16},{16,20},{20,24},{24,28},{28,0},{1,5},{5... | collective-permute-start | bytes 1572872 | tf_op jit(solution)/shard_map/ppermute | solution.py:283
  152.1 27.0 %collective-permute-start.6 = (bf16[2048,128]{1,0:T(8,128)(2,1)S(1)}, bf16[2048,128]{1,0:T(8,128)(2,1)S(1)}, u32[]{:S(2)}, u32[]{:S(2)}) collective-permute-start(bf16[2048,128]{1,0:T(8,128)(2,1)S(1)} %collective-permute-done.5), channel_id=1, source_target_pairs={{4,0},{8,4},{12,8},{16,12},{20,16},{24,20},{28,24},{0,28},{5,1},{9... | collective-permute-start | bytes 1572872 | tf_op jit(solution)/shard_map/ppermute | solution.py:285
  289.0 146.1 %reduce-scatter.5.cloned.1.call-start = ((), (), s32[]{:S(2)}) async-start(), calls=%async_computation.7 | async-start | bytes 9437184 | tf_op jit(solution)/shard_map/reduce_scatter | solution.py:255
  311.9 52.9 %collective-permute-start.8 = (bf16[256,2048]{1,0:T(8,128)(2,1)S(1)}, bf16[256,2048]{1,0:T(8,128)(2,1)S(1)}, u32[]{:S(2)}, u32[]{:S(2)}) collective-permute-start(bf16[256,2048]{1,0:T(8,128)(2,1)S(1)} %convolution_convert_fusion.13), channel_id=1, source_target_pairs={{0,1},{3,2},{4,5},{7,6},{8,9},{11,10},{12,13},{15,14},{16,17},{19,... | collective-permute-start | bytes 3145736 | tf_op jit(solution)/shard_map/ppermute | solution.py:194
  322.3 44.7 %collective-permute-start.7 = (bf16[256,2048]{1,0:T(8,128)(2,1)S(1)}, bf16[256,2048]{1,0:T(8,128)(2,1)S(1)}, u32[]{:S(2)}, u32[]{:S(2)}) collective-permute-start(bf16[256,2048]{1,0:T(8,128)(2,1)S(1)} %convolution_convert_fusion.14), channel_id=1, source_target_pairs={{0,1},{3,2},{4,5},{7,6},{8,9},{11,10},{12,13},{15,14},{16,17},{19,... | collective-permute-start | bytes 3145736 | tf_op jit(solution)/shard_map/ppermute | solution.py:194
  356.1 97.1 %collective-permute-start.11 = (bf16[256,2048]{1,0:T(8,128)(2,1)}, bf16[256,2048]{1,0:T(8,128)(2,1)}, u32[]{:S(2)}, u32[]{:S(2)}) collective-permute-start(bf16[256,2048]{1,0:T(8,128)(2,1)} %convolution_convert_fusion.11), channel_id=1, source_target_pairs={{0,1},{3,2},{4,5},{7,6},{8,9},{11,10},{12,13},{15,14},{16,17},{19,... | collective-permute-start | bytes 3145736 | tf_op jit(solution)/shard_map/ppermute | solution.py:194
  365.3 92.5 %collective-permute-start.34 = (bf16[256,2048]{1,0:T(8,128)(2,1)S(1)}, bf16[256,2048]{1,0:T(8,128)(2,1)}, u32[]{:S(2)}, u32[]{:S(2)}) collective-permute-start(bf16[256,2048]{1,0:T(8,128)(2,1)S(1)} %add.235), channel_id=1, source_target_pairs={{1,2},{2,1},{5,6},{6,5},{9,10},{10,9},{13,14},{14,13},{17,18},{18,... | collective-permute-start | bytes 3145736 | tf_op jit(solution)/shard_map/ppermute | solution.py:194
  368.3 98.2 %collective-permute-start.33 = (bf16[256,2048]{1,0:T(8,128)(2,1)}, bf16[256,2048]{1,0:T(8,128)(2,1)}, u32[]{:S(2)}, u32[]{:S(2)}) collective-permute-start(bf16[256,2048]{1,0:T(8,128)(2,1)} %add.236), channel_id=1, source_target_pairs={{1,2},{2,1},{5,6},{6,5},{9,10},{10,9},{13,14},{14,13},{17,18},{18,... | collective-permute-start | bytes 3145736 | tf_op jit(solution)/shard_map/ppermute | solution.py:194
  370.0 101.2 %collective-permute-start.10 = (bf16[256,2048]{1,0:T(8,128)(2,1)}, bf16[256,2048]{1,0:T(8,128)(2,1)}, u32[]{:S(2)}, u32[]{:S(2)}) collective-permute-start(bf16[256,2048]{1,0:T(8,128)(2,1)} %convolution_convert_fusion.12), channel_id=1, source_target_pairs={{0,1},{3,2},{4,5},{7,6},{8,9},{11,10},{12,13},{15,14},{16,17},{19,... | collective-permute-start | bytes 3145736 | tf_op jit(solution)/shard_map/ppermute | solution.py:194
  373.3 101.1 %collective-permute-start.9 = (bf16[256,2048]{1,0:T(8,128)(2,1)}, bf16[256,2048]{1,0:T(8,128)(2,1)}, u32[]{:S(2)}, u32[]{:S(2)}) collective-permute-start(bf16[256,2048]{1,0:T(8,128)(2,1)} %convolution_convert_fusion.15), channel_id=1, source_target_pairs={{0,1},{3,2},{4,5},{7,6},{8,9},{11,10},{12,13},{15,14},{16,17},{19,... | collective-permute-start | bytes 3145736 | tf_op jit(solution)/shard_map/ppermute | solution.py:194
  441.9 41.5 %all-to-all-start = ((bf16[256,8,128]{2,0,1:T(8,128)(2,1)}), bf16[256,8,128]{2,0,1:T(8,128)(2,1)}, u32[]{:S(2)}, u32[]{:S(2)}) async-start(bf16[256,8,128]{2,0,1:T(8,128)(2,1)} %bitcast.145), calls=%async_computation.2 | async-start | bytes 1048576 | tf_op jit(solution)/shard_map/all_to_all | solution.py:322
  446.0 262.3 %reduce-scatter.11.cloned.1.call-start = ((), (), s32[]{:S(2)}) async-start(), calls=%async_computation.11 | async-start | bytes 4718592 | tf_op jit(solution)/shard_map/reduce_scatter | solution.py:255
  456.2 49.4 %collective-permute-start.32 = (bf16[256,2048]{1,0:T(8,128)(2,1)}, bf16[256,2048]{1,0:T(8,128)(2,1)}, u32[]{:S(2)}, u32[]{:S(2)}) collective-permute-start(bf16[256,2048]{1,0:T(8,128)(2,1)} %add.237), channel_id=1, source_target_pairs={{1,2},{2,1},{5,6},{6,5},{9,10},{10,9},{13,14},{14,13},{17,18},{18,... | collective-permute-start | bytes 3145736 | tf_op jit(solution)/shard_map/ppermute | solution.py:194
  457.8 57.0 %collective-permute-start.14 = (bf16[256,2048]{1,0:T(8,128)(2,1)}, bf16[256,2048]{1,0:T(8,128)(2,1)}, u32[]{:S(2)}, u32[]{:S(2)}) collective-permute-start(bf16[256,2048]{1,0:T(8,128)(2,1)} %convolution_convert_fusion.9), channel_id=1, source_target_pairs={{0,1},{3,2},{4,5},{7,6},{8,9},{11,10},{12,13},{15,14},{16,17},{19,... | collective-permute-start | bytes 3145736 | tf_op jit(solution)/shard_map/ppermute | solution.py:194
  466.6 51.7 %collective-permute-start.48 = (bf16[256,2048]{1,0:T(8,128)(2,1)}, bf16[256,2048]{1,0:T(8,128)(2,1)}, u32[]{:S(2)}, u32[]{:S(2)}) collective-permute-start(bf16[256,2048]{1,0:T(8,128)(2,1)} %add.249), channel_id=1, source_target_pairs={{1,0},{2,3},{5,4},{6,7},{9,8},{10,11},{13,12},{14,15},{17,16},{18,... | collective-permute-start | bytes 3145736 | tf_op jit(solution)/shard_map/ppermute | solution.py:194
  471.2 48.0 %collective-permute-start.47 = (bf16[256,2048]{1,0:T(8,128)(2,1)}, bf16[256,2048]{1,0:T(8,128)(2,1)}, u32[]{:S(2)}, u32[]{:S(2)}) collective-permute-start(bf16[256,2048]{1,0:T(8,128)(2,1)} %add.250), channel_id=1, source_target_pairs={{1,0},{2,3},{5,4},{6,7},{9,8},{10,11},{13,12},{14,15},{17,16},{18,... | collective-permute-start | bytes 3145736 | tf_op jit(solution)/shard_map/ppermute | solution.py:194
  474.4 56.5 %collective-permute-start.31 = (bf16[256,2048]{1,0:T(8,128)(2,1)S(1)}, bf16[256,2048]{1,0:T(8,128)(2,1)}, u32[]{:S(2)}, u32[]{:S(2)}) collective-permute-start(bf16[256,2048]{1,0:T(8,128)(2,1)S(1)} %add.238), channel_id=1, source_target_pairs={{1,2},{2,1},{5,6},{6,5},{9,10},{10,9},{13,14},{14,13},{17,18},{18,... | collective-permute-start | bytes 3145736 | tf_op jit(solution)/shard_map/ppermute | solution.py:194
  483.3 356.2 %reduce-scatter.9.cloned.1.call-start = ((), (), s32[]{:S(2)}) async-start(), calls=%async_computation.10 | async-start | bytes 9437184 | tf_op jit(solution)/shard_map/reduce_scatter | solution.py:255
  505.6 31.7 %collective-permute-start.30 = (bf16[256,2048]{1,0:T(8,128)(2,1)}, bf16[256,2048]{1,0:T(8,128)(2,1)S(1)}, u32[]{:S(2)}, u32[]{:S(2)}) collective-permute-start(bf16[256,2048]{1,0:T(8,128)(2,1)} %add.239), channel_id=1, source_target_pairs={{1,2},{2,1},{5,6},{6,5},{9,10},{10,9},{13,14},{14,13},{17,18},{18,... | collective-permute-start | bytes 3145736 | tf_op jit(solution)/shard_map/ppermute | solution.py:194
  514.9 41.6 %collective-permute-start.46 = (bf16[256,2048]{1,0:T(8,128)(2,1)S(1)}, bf16[256,2048]{1,0:T(8,128)(2,1)S(1)}, u32[]{:S(2)}, u32[]{:S(2)}) collective-permute-start(bf16[256,2048]{1,0:T(8,128)(2,1)S(1)} %add.251), channel_id=1, source_target_pairs={{1,0},{2,3},{5,4},{6,7},{9,8},{10,11},{13,12},{14,15},{17,16},{18,... | collective-permute-start | bytes 3145736 | tf_op jit(solution)/shard_map/ppermute | solution.py:194
  518.3 26.1 %collective-permute-start.29 = (bf16[256,2048]{1,0:T(8,128)(2,1)S(1)}, bf16[256,2048]{1,0:T(8,128)(2,1)S(1)}, u32[]{:S(2)}, u32[]{:S(2)}) collective-permute-start(bf16[256,2048]{1,0:T(8,128)(2,1)S(1)} %add.240), channel_id=1, source_target_pairs={{1,2},{2,1},{5,6},{6,5},{9,10},{10,9},{13,14},{14,13},{17,18},{18,... | collective-permute-start | bytes 3145736 | tf_op jit(solution)/shard_map/ppermute | solution.py:194
  519.2 35.2 %collective-permute-start.13 = (bf16[256,2048]{1,0:T(8,128)(2,1)S(1)}, bf16[256,2048]{1,0:T(8,128)(2,1)S(1)}, u32[]{:S(2)}, u32[]{:S(2)}) collective-permute-start(bf16[256,2048]{1,0:T(8,128)(2,1)S(1)} %copy-done.24), channel_id=1, source_target_pairs={{0,1},{3,2},{4,5},{7,6},{8,9},{11,10},{12,13},{15,14},{16,17},{19,... | collective-permute-start | bytes 3145736 | tf_op jit(solution)/shard_map/ppermute | solution.py:194
  530.9 46.0 %collective-permute-start.12 = (bf16[256,2048]{1,0:T(8,128)(2,1)S(1)}, bf16[256,2048]{1,0:T(8,128)(2,1)S(1)}, u32[]{:S(2)}, u32[]{:S(2)}) collective-permute-start(bf16[256,2048]{1,0:T(8,128)(2,1)S(1)} %copy-done.23), channel_id=1, source_target_pairs={{0,1},{3,2},{4,5},{7,6},{8,9},{11,10},{12,13},{15,14},{16,17},{19,... | collective-permute-start | bytes 3145736 | tf_op jit(solution)/shard_map/ppermute | solution.py:194
  537.3 60.1 %collective-permute-start.17 = (bf16[256,2048]{1,0:T(8,128)(2,1)S(1)}, bf16[256,2048]{1,0:T(8,128)(2,1)S(1)}, u32[]{:S(2)}, u32[]{:S(2)}) collective-permute-start(bf16[256,2048]{1,0:T(8,128)(2,1)S(1)} %copy-done.21), channel_id=1, source_target_pairs={{0,1},{3,2},{4,5},{7,6},{8,9},{11,10},{12,13},{15,14},{16,17},{19,... | collective-permute-start | bytes 3145736 | tf_op jit(solution)/shard_map/ppermute | solution.py:194
  544.3 54.3 %collective-permute-start.45 = (bf16[256,2048]{1,0:T(8,128)(2,1)S(1)}, bf16[256,2048]{1,0:T(8,128)(2,1)S(1)}, u32[]{:S(2)}, u32[]{:S(2)}) collective-permute-start(bf16[256,2048]{1,0:T(8,128)(2,1)S(1)} %add.252), channel_id=1, source_target_pairs={{1,0},{2,3},{5,4},{6,7},{9,8},{10,11},{13,12},{14,15},{17,16},{18,... | collective-permute-start | bytes 3145736 | tf_op jit(solution)/shard_map/ppermute | solution.py:194
  554.4 53.5 %collective-permute-start.44 = (bf16[256,2048]{1,0:T(8,128)(2,1)S(1)}, bf16[256,2048]{1,0:T(8,128)(2,1)S(1)}, u32[]{:S(2)}, u32[]{:S(2)}) collective-permute-start(bf16[256,2048]{1,0:T(8,128)(2,1)S(1)} %add.253), channel_id=1, source_target_pairs={{1,0},{2,3},{5,4},{6,7},{9,8},{10,11},{13,12},{14,15},{17,16},{18,... | collective-permute-start | bytes 3145736 | tf_op jit(solution)/shard_map/ppermute | solution.py:194
  556.5 71.8 %collective-permute-start.43 = (bf16[256,2048]{1,0:T(8,128)(2,1)S(1)}, bf16[256,2048]{1,0:T(8,128)(2,1)S(1)}, u32[]{:S(2)}, u32[]{:S(2)}) collective-permute-start(bf16[256,2048]{1,0:T(8,128)(2,1)S(1)} %add.254), channel_id=1, source_target_pairs={{1,0},{2,3},{5,4},{6,7},{9,8},{10,11},{13,12},{14,15},{17,16},{18,... | collective-permute-start | bytes 3145736 | tf_op jit(solution)/shard_map/ppermute | solution.py:194
  576.9 52.9 %collective-permute-start.28 = (bf16[256,2048]{1,0:T(8,128)(2,1)S(1)}, bf16[256,2048]{1,0:T(8,128)(2,1)S(1)}, u32[]{:S(2)}, u32[]{:S(2)}) collective-permute-start(bf16[256,2048]{1,0:T(8,128)(2,1)S(1)} %add.241), channel_id=1, source_target_pairs={{1,2},{2,1},{5,6},{6,5},{9,10},{10,9},{13,14},{14,13},{17,18},{18,... | collective-permute-start | bytes 3145736 | tf_op jit(solution)/shard_map/ppermute | solution.py:194
  579.0 28.9 %copy-start.22 = (bf16[256,2048]{1,0:T(8,128)(2,1)S(1)}, bf16[256,2048]{1,0:T(8,128)(2,1)}, u32[]{:S(2)}) copy-start(bf16[256,2048]{1,0:T(8,128)(2,1)} %convolution_convert_fusion.8) | copy-start | bytes 3145732
  597.4 34.4 %collective-permute-start.27 = (bf16[256,2048]{1,0:T(8,128)(2,1)S(1)}, bf16[256,2048]{1,0:T(8,128)(2,1)S(1)}, u32[]{:S(2)}, u32[]{:S(2)}) collective-permute-start(bf16[256,2048]{1,0:T(8,128)(2,1)S(1)} %add.242), channel_id=1, source_target_pairs={{1,2},{2,1},{5,6},{6,5},{9,10},{10,9},{13,14},{14,13},{17,18},{18,... | collective-permute-start | bytes 3145736 | tf_op jit(solution)/shard_map/ppermute | solution.py:194
  598.6 36.4 %collective-permute-start.26 = (bf16[256,2048]{1,0:T(8,128)(2,1)S(1)}, bf16[256,2048]{1,0:T(8,128)(2,1)S(1)}, u32[]{:S(2)}, u32[]{:S(2)}) collective-permute-start(bf16[256,2048]{1,0:T(8,128)(2,1)S(1)} %add.243), channel_id=1, source_target_pairs={{1,2},{2,1},{5,6},{6,5},{9,10},{10,9},{13,14},{14,13},{17,18},{18,... | collective-permute-start | bytes 3145736 | tf_op jit(solution)/shard_map/ppermute | solution.py:194
  607.9 28.9 %collective-permute-start.16 = (bf16[256,2048]{1,0:T(8,128)(2,1)S(1)}, bf16[256,2048]{1,0:T(8,128)(2,1)S(1)}, u32[]{:S(2)}, u32[]{:S(2)}) collective-permute-start(bf16[256,2048]{1,0:T(8,128)(2,1)S(1)} %copy-done.22), channel_id=1, source_target_pairs={{0,1},{3,2},{4,5},{7,6},{8,9},{11,10},{12,13},{15,14},{16,17},{19,... | collective-permute-start | bytes 3145736 | tf_op jit(solution)/shard_map/ppermute | solution.py:194
  628.3 25.0 %collective-permute-start.15 = (bf16[256,2048]{1,0:T(8,128)(2,1)S(1)}, bf16[256,2048]{1,0:T(8,128)(2,1)S(1)}, u32[]{:S(2)}, u32[]{:S(2)}) collective-permute-start(bf16[256,2048]{1,0:T(8,128)(2,1)S(1)} %convolution_convert_fusion.17), channel_id=1, source_target_pairs={{0,1},{3,2},{4,5},{7,6},{8,9},{11,10},{12,13},{15,14},{16,17},{19,... | collective-permute-start | bytes 3145736 | tf_op jit(solution)/shard_map/ppermute | solution.py:194
  629.8 43.4 %collective-permute-start.20 = (bf16[256,2048]{1,0:T(8,128)(2,1)S(1)}, bf16[256,2048]{1,0:T(8,128)(2,1)S(1)}, u32[]{:S(2)}, u32[]{:S(2)}) collective-permute-start(bf16[256,2048]{1,0:T(8,128)(2,1)S(1)} %convolution_convert_fusion.6), channel_id=1, source_target_pairs={{0,1},{3,2},{4,5},{7,6},{8,9},{11,10},{12,13},{15,14},{16,17},{19,... | collective-permute-start | bytes 3145736 | tf_op jit(solution)/shard_map/ppermute | solution.py:194
  631.7 48.7 %collective-permute-start.42 = (bf16[256,2048]{1,0:T(8,128)(2,1)S(1)}, bf16[256,2048]{1,0:T(8,128)(2,1)S(1)}, u32[]{:S(2)}, u32[]{:S(2)}) collective-permute-start(bf16[256,2048]{1,0:T(8,128)(2,1)S(1)} %add.255), channel_id=1, source_target_pairs={{1,0},{2,3},{5,4},{6,7},{9,8},{10,11},{13,12},{14,15},{17,16},{18,... | collective-permute-start | bytes 3145736 | tf_op jit(solution)/shard_map/ppermute | solution.py:194
  635.0 52.6 %collective-permute-start.41 = (bf16[256,2048]{1,0:T(8,128)(2,1)S(1)}, bf16[256,2048]{1,0:T(8,128)(2,1)S(1)}, u32[]{:S(2)}, u32[]{:S(2)}) collective-permute-start(bf16[256,2048]{1,0:T(8,128)(2,1)S(1)} %add.256), channel_id=1, source_target_pairs={{1,0},{2,3},{5,4},{6,7},{9,8},{10,11},{13,12},{14,15},{17,16},{18,... | collective-permute-start | bytes 3145736 | tf_op jit(solution)/shard_map/ppermute | solution.py:194
  636.7 66.3 %collective-permute-start.40 = (bf16[256,2048]{1,0:T(8,128)(2,1)S(1)}, bf16[256,2048]{1,0:T(8,128)(2,1)S(1)}, u32[]{:S(2)}, u32[]{:S(2)}) collective-permute-start(bf16[256,2048]{1,0:T(8,128)(2,1)S(1)} %add.257), channel_id=1, source_target_pairs={{1,0},{2,3},{5,4},{6,7},{9,8},{10,11},{13,12},{14,15},{17,16},{18,... | collective-permute-start | bytes 3145736 | tf_op jit(solution)/shard_map/ppermute | solution.py:194
  653.4 45.6 %collective-permute-start.25 = (bf16[256,2048]{1,0:T(8,128)(2,1)S(1)}, bf16[256,2048]{1,0:T(8,128)(2,1)S(1)}, u32[]{:S(2)}, u32[]{:S(2)}) collective-permute-start(bf16[256,2048]{1,0:T(8,128)(2,1)S(1)} %add.244), channel_id=1, source_target_pairs={{1,2},{2,1},{5,6},{6,5},{9,10},{10,9},{13,14},{14,13},{17,18},{18,... | collective-permute-start | bytes 3145736 | tf_op jit(solution)/shard_map/ppermute | solution.py:194
  654.1 27.0 %slice-start = ((s8[8388608]{0:T(1024)(128)(4,1)}), s8[4194304]{0:T(1024)(128)(4,1)S(1)}, s32[]{:S(2)}) async-start(s8[8388608]{0:T(1024)(128)(4,1)} %bitcast.128), calls=%async_computation.12 | async-start | bytes 8388608
  673.2 29.8 %collective-permute-start.24 = (bf16[256,2048]{1,0:T(8,128)(2,1)S(1)}, bf16[256,2048]{1,0:T(8,128)(2,1)S(1)}, u32[]{:S(2)}, u32[]{:S(2)}) collective-permute-start(bf16[256,2048]{1,0:T(8,128)(2,1)S(1)} %add.245), channel_id=1, source_target_pairs={{1,2},{2,1},{5,6},{6,5},{9,10},{10,9},{13,14},{14,13},{17,18},{18,... | collective-permute-start | bytes 3145736 | tf_op jit(solution)/shard_map/ppermute | solution.py:194
  680.4 25.3 %collective-permute-start.23 = (bf16[256,2048]{1,0:T(8,128)(2,1)S(1)}, bf16[256,2048]{1,0:T(8,128)(2,1)S(1)}, u32[]{:S(2)}, u32[]{:S(2)}) collective-permute-start(bf16[256,2048]{1,0:T(8,128)(2,1)S(1)} %add.246), channel_id=1, source_target_pairs={{1,2},{2,1},{5,6},{6,5},{9,10},{10,9},{13,14},{14,13},{17,18},{18,... | collective-permute-start | bytes 3145736 | tf_op jit(solution)/shard_map/ppermute | solution.py:194
  687.6 52.3 %collective-permute-start.18 = (bf16[2048,384]{1,0:T(8,128)(2,1)}, bf16[2048,384]{1,0:T(8,128)(2,1)}, u32[]{:S(2)}, u32[]{:S(2)}) collective-permute-start(bf16[2048,384]{1,0:T(8,128)(2,1)} %convolution_convert_fusion.4), channel_id=1, source_target_pairs={{0,1},{3,2},{4,5},{7,6},{8,9},{11,10},{12,13},{15,14},{16,17},{19,... | collective-permute-start | bytes 4718600 | tf_op jit(solution)/shard_map/ppermute | solution.py:194
  700.3 30.8 %collective-permute-start.39 = (bf16[256,2048]{1,0:T(8,128)(2,1)}, bf16[256,2048]{1,0:T(8,128)(2,1)}, u32[]{:S(2)}, u32[]{:S(2)}) collective-permute-start(bf16[256,2048]{1,0:T(8,128)(2,1)} %add.258), channel_id=1, source_target_pairs={{1,0},{2,3},{5,4},{6,7},{9,8},{10,11},{13,12},{14,15},{17,16},{18,... | collective-permute-start | bytes 3145736 | tf_op jit(solution)/shard_map/ppermute | solution.py:194
  704.4 46.7 %collective-permute-start.38 = (bf16[256,2048]{1,0:T(8,128)(2,1)}, bf16[256,2048]{1,0:T(8,128)(2,1)}, u32[]{:S(2)}, u32[]{:S(2)}) collective-permute-start(bf16[256,2048]{1,0:T(8,128)(2,1)} %add.259), channel_id=1, source_target_pairs={{1,0},{2,3},{5,4},{6,7},{9,8},{10,11},{13,12},{14,15},{17,16},{18,... | collective-permute-start | bytes 3145736 | tf_op jit(solution)/shard_map/ppermute | solution.py:194
  707.0 62.2 %collective-permute-start.37 = (bf16[256,2048]{1,0:T(8,128)(2,1)}, bf16[256,2048]{1,0:T(8,128)(2,1)}, u32[]{:S(2)}, u32[]{:S(2)}) collective-permute-start(bf16[256,2048]{1,0:T(8,128)(2,1)} %add.260), channel_id=1, source_target_pairs={{1,0},{2,3},{5,4},{6,7},{9,8},{10,11},{13,12},{14,15},{17,16},{18,... | collective-permute-start | bytes 3145736 | tf_op jit(solution)/shard_map/ppermute | solution.py:194
  708.4 30.3 %collective-permute-start.19 = (bf16[128,2048]{1,0:T(8,128)(2,1)}, bf16[128,2048]{1,0:T(8,128)(2,1)S(1)}, u32[]{:S(2)}, u32[]{:S(2)}) collective-permute-start(bf16[128,2048]{1,0:T(8,128)(2,1)} %reduce-scatter.11.cloned.1.call-done), channel_id=1, source_target_pairs={{0,1},{3,2},{4,5},{7,6},{8,9},{11,10},{12,13},{15,14},{16,17},{19,... | collective-permute-start | bytes 1572872 | tf_op jit(solution)/shard_map/ppermute | solution.py:194
  742.2 31.8 %collective-permute-start.21 = (bf16[2048,384]{1,0:T(8,128)(2,1)S(1)}, bf16[2048,384]{1,0:T(8,128)(2,1)S(1)}, u32[]{:S(2)}, u32[]{:S(2)}) collective-permute-start(bf16[2048,384]{1,0:T(8,128)(2,1)S(1)} %add.248), channel_id=1, source_target_pairs={{1,2},{2,1},{5,6},{6,5},{9,10},{10,9},{13,14},{14,13},{17,18},{18,... | collective-permute-start | bytes 4718600 | tf_op jit(solution)/shard_map/ppermute | solution.py:194
  769.2 3.3 collective-permute-start.22
  772.6 33.5 %collective-permute-start.36 = (bf16[128,2048]{1,0:T(8,128)(2,1)S(1)}, bf16[128,2048]{1,0:T(8,128)(2,1)S(1)}, u32[]{:S(2)}, u32[]{:S(2)}) collective-permute-start(bf16[128,2048]{1,0:T(8,128)(2,1)S(1)} %add.261), channel_id=1, source_target_pairs={{1,0},{2,3},{5,4},{6,7},{9,8},{10,11},{13,12},{14,15},{17,16},{18,... | collective-permute-start | bytes 1572872 | tf_op jit(solution)/shard_map/ppermute | solution.py:194
  775.5 60.7 %collective-permute-start.35 = (bf16[2048,384]{1,0:T(8,128)(2,1)}, bf16[2048,384]{1,0:T(8,128)(2,1)}, u32[]{:S(2)}, u32[]{:S(2)}) collective-permute-start(bf16[2048,384]{1,0:T(8,128)(2,1)} %add.262), channel_id=1, source_target_pairs={{1,0},{2,3},{5,4},{6,7},{9,8},{10,11},{13,12},{14,15},{17,16},{18,... | collective-permute-start | bytes 4718600 | tf_op jit(solution)/shard_map/ppermute | solution.py:194
  (68 other events, 409.7 us)
Sparse Core Ops, SparseCore 0:
  9.9 57.0 all-gather.3
  68.9 40.9 all-gather.5
  111.8 73.2 all-gather.7
  289.1 70.3 reduce-scatter.6
  363.8 71.2 reduce-scatter.4
  483.4 55.6 reduce-scatter.10
  543.0 71.2 reduce-scatter.8
